TPU v7x, 768 devices: a whole 4x8x12 slice. The times are simulated.
768 devices in a mesh: tile: 32 (over x_hi, y, core), trc: 24 (over x_lo, z).
Axes of the slice: x: 4 (x_hi: 2, x_lo: 2; x = x_hi * 2 + x_lo), y: 8, z: 12, core: 2. Of those that a mesh axis runs over, the one named last changes fastest.
Arguments:
- tracers: float32 [96, 8, 256, 128], P('trc', None, 'tile'), may hold values from -6 to 6
- flux_pool: float32 [24, 2, 3, 8, 256, 128], P('trc', None, None, None, 'tile'), may hold values from -0.45 to 0.45
- mass_pool: float32 [24, 2, 8, 256, 128], P('trc', None, None, 'tile'), may hold values from 1 to 2
- owner: int32 [2, 32], P(None, 'tile'), may hold values from 0 to 23
- conv_cols: int32 [32, 256], P('tile'), may hold values from 0 to 1023, as said below
- conv_steps: int32 [32, 256], P('tile'), may hold values from 1 to 3
- conv_rate: float32 [32, 7, 256], P('tile'), may hold values from 0.05 to 0.5
Outputs:
- advected: float32 [96, 8, 256, 128], P('trc', None, 'tile')
Inputs may be any that keep to these rules, and one draw needn't show every extreme that they name: `conv_cols`: the 256 columns listed for one tile are all different.
All inputs are finite; a program needn't handle non-finite values.
Results may differ from a plain program's by a relative error of at most 0.0003.
Values sent between devices are 32-bit elements; how exact they have to be, the bound alone decides.
No kernel may reach another device: no remote copies, remote signals or barrier semaphores. Data moves between devices by JAX's collectives and lax.ppermute only.
A program may use at most 32 MiB of HBM per device.

v0:
```python
import jax
import jax.numpy as jnp
from jax import lax
from jax.sharding import PartitionSpec as P


def from_root(block, axis, source):
    block = jnp.where(lax.axis_index(axis) == source, block, jnp.zeros_like(block))
    return lax.psum(block, axis)


def padded_2(x, sides, width):
    for axis, dim in sides:
        size, length = (lax.axis_size(axis), x.shape[dim])
        up = [(i, (i + 1) % size) for i in range(size)]
        down = [(j, i) for i, j in up]
        last = lax.slice_in_dim(x, length - width, length, axis=dim)
        initial = lax.slice_in_dim(x, 0, width, axis=dim)
        before = lax.ppermute(last, axis, up)
        after = lax.ppermute(initial, axis, down)
        x = jnp.concatenate([before, x, after], axis=dim)
    return x


def slab(values_in, first_index, how_many, along):
    position = along % values_in.ndim
    return lax.slice_in_dim(values_in, first_index, first_index + how_many, axis=position)


def pad_axis(values_in, along, pad_low, pad_high, pad_mode):
    widths = [(0, 0)] * values_in.ndim
    widths[along % values_in.ndim] = (pad_low, pad_high)
    return jnp.pad(values_in, widths, mode=pad_mode)


def closed_faces(face_flux, along):
    position = along % face_flux.ndim
    face_count = face_flux.shape[position]
    dims_shape = [1] * face_flux.ndim
    dims_shape[position] = face_count
    kept_mask = (jnp.arange(face_count) < face_count - 1).reshape(dims_shape)
    return jnp.where(kept_mask, face_flux, 0.0)


def parabola_sweep(padded, mass_pad, face_flux, along, length):
    count_edges = length + 3
    outer_left = slab(padded, 0, count_edges, along)
    inner_left = slab(padded, 1, count_edges, along)
    inner_right = slab(padded, 2, count_edges, along)
    outer_right = slab(padded, 3, count_edges, along)
    edge_values = 7.0 / 12.0 * (inner_left + inner_right) - 1.0 / 12.0 * (outer_left + outer_right)
    edge_values = jnp.clip(
        edge_values, jnp.minimum(inner_left, inner_right), jnp.maximum(inner_left, inner_right)
    )
    count_cells = length + 2
    centre = slab(padded, 2, count_cells, along)
    left_edge = slab(edge_values, 0, count_cells, along)
    right_edge = slab(edge_values, 1, count_cells, along)
    extremum = (right_edge - centre) * (centre - left_edge) <= 0.0
    left_edge = jnp.where(extremum, centre, left_edge)
    right_edge = jnp.where(extremum, centre, right_edge)
    edge_jump = right_edge - left_edge
    curvature = 6.0 * (centre - 0.5 * (left_edge + right_edge))
    new_left = jnp.where(
        edge_jump * curvature > edge_jump * edge_jump, 3.0 * centre - 2.0 * right_edge, left_edge
    )
    new_right = jnp.where(
        -edge_jump * edge_jump > edge_jump * curvature, 3.0 * centre - 2.0 * left_edge, right_edge
    )
    edge_jump = new_right - new_left
    curvature = 6.0 * (centre - 0.5 * (new_left + new_right))
    face_count = length + 1
    upwind_mass = slab(mass_pad, 0, face_count, along)
    downwind_mass = slab(mass_pad, 1, face_count, along)
    forward = jnp.maximum(face_flux, 0.0) / upwind_mass
    backward = jnp.maximum(-face_flux, 0.0) / downwind_mass
    from_left = slab(new_right, 0, face_count, along) - 0.5 * forward * (
        slab(edge_jump, 0, face_count, along)
        - (1.0 - forward * (2.0 / 3.0)) * slab(curvature, 0, face_count, along)
    )
    from_right = slab(new_left, 1, face_count, along) + 0.5 * backward * (
        slab(edge_jump, 1, face_count, along)
        + (1.0 - backward * (2.0 / 3.0)) * slab(curvature, 1, face_count, along)
    )
    transport = face_flux * jnp.where(face_flux > 0.0, from_left, from_right)
    interior = slab(padded, 3, length, along)
    air_mass = slab(mass_pad, 1, length, along)
    return (
        interior
        - (slab(transport, 1, length, along) - slab(transport, 0, length, along)) / air_mass
    )


def local_sweep(tracer, face_flux, air_mass, along):
    length = tracer.shape[along]
    return parabola_sweep(
        pad_axis(tracer, along, 3, 3, "edge"),
        pad_axis(air_mass, along, 1, 1, "edge"),
        pad_axis(closed_faces(face_flux, along), along, 1, 0, "constant"),
        along,
        length,
    )


def convect(columns, rates, level_axis):
    lower_levels = slab(columns, 0, columns.shape[level_axis] - 1, level_axis)
    moved = rates * lower_levels
    return (
        columns
        + pad_axis(moved, level_axis, 1, 0, "constant")
        - pad_axis(moved, level_axis, 0, 1, "constant")
    )


def dense_convection(column_ids, step_counts, rates, cell_total):
    dense_rates = jnp.zeros((rates.shape[0], cell_total), jnp.float32).at[:, column_ids].set(rates)
    dense_steps = jnp.zeros((cell_total,), jnp.int32).at[column_ids].set(step_counts)
    return (dense_rates, dense_steps)


def convect_device(state, dense_rates, dense_steps):
    flattened = state.reshape(state.shape[0], state.shape[1], -1)
    for substep in range(3):
        flattened = jnp.where(dense_steps > substep, convect(flattened, dense_rates, -2), flattened)
    return flattened.reshape(state.shape)


def body(tracers, flux_pool, mass_pool, owner, conv_cols, conv_steps, conv_rate):
    tracer_count = tracers.shape[0]
    cells_x = tracers.shape[2]
    steps_total = flux_pool.shape[1]
    dense_rates, dense_steps = dense_convection(
        conv_cols[0], conv_steps[0], conv_rate[0], tracers.shape[2] * tracers.shape[3]
    )
    state = tracers
    for moment in range(steps_total):
        own_fields = jnp.concatenate((flux_pool[0, moment], mass_pool[0, moment][None]), axis=0)
        meteo = from_root(own_fields, "trc", owner[moment, 0])
        joined = jnp.concatenate((state, meteo[0][None], meteo[3][None]), axis=0)
        joined_halo = padded_2(joined, (("tile", 2),), 3)
        tracer_halo = joined_halo[:tracer_count]
        met_halo = joined_halo[tracer_count:]
        rim_width = 3
        x_flux = slab(met_halo[0], rim_width - 1, cells_x + 1, -2)
        mass_pad = slab(met_halo[1], rim_width - 1, cells_x + 2, -2)
        state = parabola_sweep(tracer_halo, mass_pad, x_flux, -2, cells_x)
        state = local_sweep(state, meteo[1], meteo[3], -1)
        state = local_sweep(state, meteo[2], meteo[3], -3)
        state = convect_device(state, dense_rates, dense_steps)
    return state


def solution(mesh):
    in_specs = (
        P("trc", None, "tile", None),
        P("trc", None, None, None, "tile", None),
        P("trc", None, None, "tile", None),
        P(None, "tile"),
        P("tile", None),
        P("tile", None),
        P("tile", None, None),
    )
    out_specs = P("trc", None, "tile", None)
    return jax.shard_map(body, mesh=mesh, in_specs=in_specs, out_specs=out_specs, check_vma=False)
```

profile of v0, /device:TPU:57, one launch (start us, length us, event | category | flops | bytes accessed | tf_op | source)
XLA Modules:
  0.0 259.7 jit_solution(2650043916081812002)
XLA Ops:
  6.5 0.7 copy-done.4
  7.2 0.6 fusion.129
  9.1 1.0 slice_bitcast_fusion
  10.1 0.7 maximum_select_fusion
  10.9 0.7 copy-done.5
  11.7 1.3 scatter_custom_fusion.1
  13.2 1.6 scatter_custom_fusion
  14.7 184.5 %all-reduce.19.cloned.1.call-done = (f32[4,8,8,128]{3,2,1,0:T(8,128)}, f32[4,8,8,128]{3,2,1,0:T(8,128)}) async-done(((f32[4,8,8,128]{3,2,1,0:T(8,128)}, f32[4,8,8,128]{3,2,1,0:T(8,128)}), (f32[4,8,8,128]{3,2,1,0:T(8,128)}, f32[4,8,8,128]{3,2,1,0:T(8,128)})) %all-reduce.19.cloned.1.call-update) | async-done | bytes 262160 | tf_op jit(solution)/shard_map/psum | solution.py:9
  199.2 0.8 slice_bitcast_fusion.17
  200.1 0.9 fusion.111
  201.2 0.7 slice_bitcast_fusion.15
  202.1 0.7 copy-done
  202.9 21.4 %collective-permute-start = (f32[6,8,3,128]{3,1,2,0:T(8,128)S(1)}, f32[6,8,3,128]{3,1,2,0:T(8,128)S(1)}, u32[]{:S(2)}, u32[]{:S(2)}) collective-permute-start(f32[6,8,3,128]{3,1,2,0:T(8,128)S(1)} %get-tuple-element.31), channel_id=1, source_target_pairs={{0,24},{24,48},{48,72},{72,96},{96,120},{120,144},{144,168},{168,1... | collective-permute-start | bytes 221192 | tf_op jit(solution)/shard_map/ppermute | solution.py:19
  224.3 1.9 collective-permute-start.1
  227.3 6.3 %collective-permute-done.1 = f32[6,8,3,128]{3,1,2,0:T(8,128)S(1)} collective-permute-done((f32[6,8,3,128]{3,1,2,0:T(8,128)S(1)}, f32[6,8,3,128]{3,1,2,0:T(8,128)S(1)}, u32[]{:S(2)}, u32[]{:S(2)}) %collective-permute-start.1) | collective-permute-done | bytes 73760 | tf_op jit(solution)/shard_map/ppermute | solution.py:20
  235.0 0.3 fusion.39
  235.3 0.3 fusion.119
  235.8 0.3 fusion.32
  237.3 1.9 collective-permute-start.2
  239.3 2.4 collective-permute-start.3
  241.8 6.8 %collective-permute-done.3 = f32[6,8,3,128]{3,1,2,0:T(8,128)S(1)} collective-permute-done((f32[6,8,3,128]{3,1,2,0:T(8,128)S(1)}, f32[6,8,3,128]{3,1,2,0:T(8,128)S(1)}, u32[]{:S(2)}, u32[]{:S(2)}) %collective-permute-start.3) | collective-permute-done | bytes 73760 | tf_op jit(solution)/shard_map/ppermute | solution.py:20
  250.0 0.3 fusion.47
  250.3 0.3 fusion.116
  252.2 0.7 copy.330
  (140 shorter events, 7.3 us)
Async XLA Ops:
  6.5 192.7 %all-reduce.19.cloned.1.call-start = ((), (), s32[]{:S(2)}) async-start(), calls=%async_computation | async-start | bytes 524288 | tf_op jit(solution)/shard_map/psum | solution.py:9
  6.5 0.7 copy-start.4
  9.1 1.0 copy-start.2
  10.8 0.7 copy-start.3
  10.8 0.7 copy-start.5
  199.2 0.9 copy-start.1
  201.9 0.9 copy-start
  202.9 24.3 %collective-permute-start = (f32[6,8,3,128]{3,1,2,0:T(8,128)S(1)}, f32[6,8,3,128]{3,1,2,0:T(8,128)S(1)}, u32[]{:S(2)}, u32[]{:S(2)}) collective-permute-start(f32[6,8,3,128]{3,1,2,0:T(8,128)S(1)} %get-tuple-element.31), channel_id=1, source_target_pairs={{0,24},{24,48},{48,72},{72,96},{96,120},{120,144},{144,168},{168,1... | collective-permute-start | bytes 221192 | tf_op jit(solution)/shard_map/ppermute | solution.py:19
  224.3 9.3 %collective-permute-start.1 = (f32[6,8,3,128]{3,1,2,0:T(8,128)S(1)}, f32[6,8,3,128]{3,1,2,0:T(8,128)S(1)}, u32[]{:S(2)}, u32[]{:S(2)}) collective-permute-start(f32[6,8,3,128]{3,1,2,0:T(8,128)S(1)} %get-tuple-element.32), channel_id=1, source_target_pairs={{24,0},{48,24},{72,48},{96,72},{120,96},{144,120},{168,144},{192,1... | collective-permute-start | bytes 221192 | tf_op jit(solution)/shard_map/ppermute | solution.py:20
  237.3 4.4 %collective-permute-start.2 = (f32[6,8,3,128]{3,1,2,0:T(8,128)S(1)}, f32[6,8,3,128]{3,1,2,0:T(8,128)S(1)}, u32[]{:S(2)}, u32[]{:S(2)}) collective-permute-start(f32[6,8,3,128]{3,1,2,0:T(8,128)S(1)} %get-tuple-element.29), channel_id=1, source_target_pairs={{0,24},{24,48},{48,72},{72,96},{96,120},{120,144},{144,168},{168,1... | collective-permute-start | bytes 221192 | tf_op jit(solution)/shard_map/ppermute | solution.py:19
  239.3 9.3 %collective-permute-start.3 = (f32[6,8,3,128]{3,1,2,0:T(8,128)S(1)}, f32[6,8,3,128]{3,1,2,0:T(8,128)S(1)}, u32[]{:S(2)}, u32[]{:S(2)}) collective-permute-start(f32[6,8,3,128]{3,1,2,0:T(8,128)S(1)} %get-tuple-element.30), channel_id=1, source_target_pairs={{24,0},{48,24},{72,48},{96,72},{120,96},{144,120},{168,144},{192,1... | collective-permute-start | bytes 221192 | tf_op jit(solution)/shard_map/ppermute | solution.py:20
Sparse Core Ops, SparseCore 0:
  11.0 188.2 all-reduce.18
where the time goes:
time: 260 us
  waiting for transfers between devices  198 us (76%)
  starting transfers between devices  27.6 us (11%)
  between operations  15.6 us (6%)
  local copies, waits for them, and re-layouts  11.8 us (5%)
  other arithmetic  7.12 us (3%)
    psum x1, waiting for transfers between devices, from_root(): return lax.psum(block, axis)  184 us
    ppermute x2, starting transfers between devices, padded_2(): before = lax.ppermute(last, axis, up)  23.3 us
    ppermute x2, waiting for transfers between devices, padded_2(): after = lax.ppermute(initial, axis, down)  13.1 us
  transfers between devices with their start and end apart: 5, of which 3 were waited for; matrix products, arithmetic and copies ran while one was open for 2% of the time, Pallas kernels for 0%

commit v1 on v0

v1 whole, which is shorter than its diff:
```python
import jax
import jax.numpy as jnp
from jax import lax
from jax.experimental import pallas as pl
from jax.experimental.pallas import tpu as pltpu
from jax.sharding import Mesh, PartitionSpec as P

TILE = ("x_hi", "y", "core")
TRC = ("x_lo", "za", "zb")
VM = pl.BlockSpec(memory_space=pltpu.VMEM)
F32 = jnp.float32


def shaped(*shape):
    return jax.ShapeDtypeStruct(shape, F32)


def call(kernel, outs, *args, scratch=(), flops=20000, name=None):
    size = sum(4 * a.size for a in args)
    return pl.pallas_call(
        kernel,
        out_shape=outs,
        in_specs=[VM] * len(args),
        out_specs=jax.tree.map(lambda _: VM, outs),
        scratch_shapes=list(scratch),
        cost_estimate=pl.CostEstimate(flops=flops, bytes_accessed=size, transcendentals=0),
        name=name,
    )(*args)


def column(ref, first, x):
    return ref[pl.ds(first + x, 8, stride=8), :]


def pack_kernel(flux_ref, mass_ref, owner_ref, out_ref, owner_out):
    for s in range(2):
        for x in range(8):
            for f in range(3):
                out_ref[f, s, x] = column(flux_ref, (s * 3 + f) * 64, x)
            out_ref[3, s, x] = column(mass_ref, s * 64, x)
        owner_out[s] = jnp.broadcast_to(owner_ref[s : s + 1, 0:1], (8, 128))


def pick_member_kernel(owner_ref, got_ref, out_ref):
    for s in range(2):
        owner = owner_ref[s]
        member = 2 * (owner // 12) + (owner % 2)
        masks = [member == m for m in range(3)]
        for x in range(8):
            value = got_ref[3, s, x]
            for m in range(3):
                value = jnp.where(masks[m], got_ref[m, s, x], value)
            out_ref[s, x] = value


def pick_pair_kernel(owner_ref, got_ref, out_ref):
    for s in range(2):
        pair = (owner_ref[s] % 12) // 2
        masks = [pair == p for p in range(5)]
        for b in range(2):
            for x in range(8):
                value = got_ref[5, b, s, x]
                for p in range(5):
                    value = jnp.where(masks[p], got_ref[p, b, s, x], value)
                out_ref[b, s, x] = value


def convection_kernel(cols_ref, steps_ref, rate_ref, out_ref):
    cols = cols_ref[...]
    at_x, at_y = cols // 128, cols % 128
    values = jnp.concatenate([steps_ref[...].astype(F32), rate_ref[...]], axis=0)
    weights = jnp.concatenate([jnp.where(at_x == x, values, 0.0) for x in range(8)], axis=0)
    hot = jnp.where(lax.broadcasted_iota(jnp.int32, (128, cols.shape[1]), 0) == at_y, 1.0, 0.0)
    dense = lax.dot_general(
        weights, hot, (((1,), (1,)), ((), ())),
        precision=lax.Precision.HIGHEST, preferred_element_type=F32,
    )
    out_ref[...] = dense.reshape(out_ref.shape)


FX, FY, FZ, MASS = range(4)
RIGHT = [(FX, 0, (4, 5, 6, 7)), (MASS, 0, (4, 5, 6, 7)), (FY, 0, (5, 6, 7)), (FZ, 0, (5, 6, 7)), (FX, 1, (7,)), (MASS, 1, (7,))]
LEFT = [(FX, 0, (0, 1, 2)), (MASS, 0, (0, 1, 2, 3)), (FY, 0, (0, 1, 2)), (FZ, 0, (0, 1, 2)), (MASS, 1, (0,))]


def places(plan, offset):
    at, where = 24, {}
    for field, step, columns in plan:
        for x in columns:
            where[field, step, x + offset] = at
            at += 1
    return where, at


FROM_LEFT, CONV_FROM_LEFT = places(RIGHT, -8)
FROM_RIGHT, CONV_FROM_RIGHT = places(LEFT, 8)


def send_kernel(met_ref, tracers_ref, conv_ref, right_ref, left_ref):
    for i in range(4):
        for n in range(6):
            right_ref[6 * i + n] = column(tracers_ref, 64 * i, 2 + n)
            left_ref[6 * i + n] = column(tracers_ref, 64 * i, n)
    for plan, out, conv_columns in ((RIGHT, right_ref, (5, 6, 7)), (LEFT, left_ref, (0, 1, 2))):
        at = 24
        for field, step, columns in plan:
            for x in columns:
                out[at] = met_ref[field, step, x]
                at += 1
        for x in conv_columns:
            out[at] = conv_ref[x]
            at += 1


def clipped(value, bound):
    return jnp.maximum(jnp.minimum(value, jnp.maximum(bound, 0.0)), jnp.minimum(bound, 0.0))


def edge_offset(before, here, after):
    return clipped(0.5 * here + (1.0 / 12.0) * (before - after), here)


def limited(u, v):
    return clipped(u, v + v), clipped(v, u + u)


def face_factors(flux, near, far):
    size = jnp.abs(flux)
    share = size * jnp.where(flux > 0.0, near, far)
    rest = size * (1.0 - share)
    return rest * (1.0 - share), rest * share


def line_sweep(q, flux, k1, k2, per_mass, open_face, axis):
    length = q.shape[axis]

    def ahead(x):
        return pltpu.roll(x, length - 1, axis)

    def behind(x):
        return pltpu.roll(x, 1, axis)

    q_next = ahead(q)
    diff = jnp.where(open_face, q_next - q, 0.0)
    u = edge_offset(behind(diff), diff, ahead(diff))
    v = behind(diff - u)
    u, v = limited(u, v)
    forward = flux > 0.0
    transport = (
        flux * jnp.where(forward, q, q_next)
        + k1 * jnp.where(forward, u, ahead(v))
        + k2 * jnp.where(forward, v, ahead(u))
    )
    return q - (transport - behind(transport)) * per_mass


def sweeps_kernel(met_ref, tracers_ref, conv_ref, left_ref, right_ref, out_ref, state, swept, factors, per_mass, lines):
    lane = lax.broadcasted_iota(jnp.int32, (8, 128), 1)
    level = lax.broadcasted_iota(jnp.int32, (8, 128), 0)
    open_y, open_z = lane < 127, level < 7

    def met(field, step, x):
        if x < 0:
            return left_ref[FROM_LEFT[field, step, x]]
        if x > 7:
            return right_ref[FROM_RIGHT[field, step, x]]
        return met_ref[field, step, x]

    def dense(x):
        if x < 0:
            return left_ref[CONV_FROM_LEFT + 3 + x]
        if x > 7:
            return right_ref[CONV_FROM_RIGHT + x - 8]
        return conv_ref[x]

    def tracer(i, x):
        if x < 0:
            return left_ref[6 * i + 6 + x]
        if x > 7:
            return right_ref[6 * i + x - 8]
        return column(tracers_ref, 64 * i, x)

    for step in range(2):
        lo, hi = (-3, 10) if step == 0 else (0, 7)
        count = hi - lo + 1
        for n in range(count + 2):
            per_mass[n] = 1.0 / met(MASS, step, lo - 1 + n)
        for n in range(count + 1):
            flux = met(FX, step, lo - 1 + n)
            k1, k2 = face_factors(flux, per_mass[n], per_mass[n + 1])
            factors[0, n], factors[1, n], factors[2, n] = flux, k1, k2
        for n in range(count):
            lines[0, n] = met(FY, step, lo + n)
            lines[1, n] = met(FZ, step, lo + n)
            lines[2, n] = dense(lo + n)

        for i in range(4):
            q, diff, u, v, sent = {}, {}, {}, {}, {}
            for e in range(lo - 3, hi + 4):
                q[e] = tracer(i, e) if step == 0 else state[i, e + 3]
                if e - 1 in q:
                    diff[e - 1] = q[e] - q[e - 1]
                if e - 3 in diff:
                    u[e - 2] = edge_offset(diff[e - 3], diff[e - 2], diff[e - 1])
                    v[e - 1] = diff[e - 2] - u[e - 2]
                j = e - 2
                if j in v:
                    u[j], v[j] = limited(u[j], v[j])
                j = e - 3
                if lo - 1 <= j <= hi:
                    n = j - lo + 1
                    flux = factors[0, n]
                    forward = flux > 0.0
                    sent[j] = (
                        flux * jnp.where(forward, q[j], q[j + 1])
                        + factors[1, n] * jnp.where(forward, u[j], v[j + 1])
                        + factors[2, n] * jnp.where(forward, v[j], u[j + 1])
                    )
                if lo <= j <= hi:
                    swept[i, j - lo] = q[j] - (sent[j] - sent[j - 1]) * per_mass[j - lo + 1]

        def across(block, _):
            for m in range(2):
                n = 2 * block + m
                r = per_mass[n + 1]
                fy = jnp.where(open_y, lines[0, n], 0.0)
                y1, y2 = face_factors(fy, r, pltpu.roll(r, 127, 1))
                fz = jnp.where(open_z, lines[1, n], 0.0)
                z1, z2 = face_factors(fz, r, pltpu.roll(r, 7, 0))
                table = lines[2, n]
                substeps = jnp.broadcast_to(table[0:1, :], (8, 128))
                rate = jnp.where(level > 0, table, 0.0)
                rates = [jnp.where(substeps > least, rate, 0.0) for least in (0.5, 1.5, 2.5)]
                keeps = [1.0 - pltpu.roll(part, 7, 0) for part in rates]
                for i in range(4):
                    q = swept[i, n]
                    q = line_sweep(q, fy, y1, y2, r, open_y, 1)
                    q = line_sweep(q, fz, z1, z2, r, open_z, 0)
                    for part, keep in zip(rates, keeps):
                        q = q * keep + part * pltpu.roll(q, 1, 0)
                    if step == 0:
                        state[i, n] = q
                    else:
                        out_ref[pl.ds(64 * i + n, 8, stride=8), :] = q
            return 0

        lax.fori_loop(0, count // 2, across, 0)


def body(tracers, flux_pool, mass_pool, owner, conv_cols, conv_steps, conv_rate):
    packed, owners = call(
        pack_kernel, (shaped(4, 2, 8, 8, 128), jax.ShapeDtypeStruct((2, 8, 128), jnp.int32)),
        flux_pool.reshape(384, 128), mass_pool.reshape(128, 128), owner, name="pack",
    )
    members = lax.all_to_all(packed, ("x_lo", "zb"), 0, 0, tiled=False)
    dense = call(
        convection_kernel, shaped(8, 8, 128), conv_cols, conv_steps, conv_rate[0], flops=30000000, name="convection",
    )
    mine = call(pick_member_kernel, shaped(2, 8, 8, 128), owners, members, name="pick_member")
    pairs = lax.all_gather(mine, ("za", "zb")).reshape(6, 2, 2, 8, 8, 128)
    half = call(pick_pair_kernel, shaped(2, 2, 8, 8, 128), owners, pairs, name="pick_pair")
    met = lax.all_gather(half, "x_lo").reshape(4, 2, 8, 8, 128)
    lines = tracers.reshape(256, 128)
    to_right, to_left = call(
        send_kernel, (shaped(CONV_FROM_LEFT + 3, 8, 128), shaped(CONV_FROM_RIGHT + 3, 8, 128)), met, lines, dense, name="send",
    )
    size = lax.axis_size(TILE)
    up = [(i, (i + 1) % size) for i in range(size)]
    from_left = lax.ppermute(to_right, TILE, up)
    from_right = lax.ppermute(to_left, TILE, [(b, a) for a, b in up])
    out = call(
        sweeps_kernel, shaped(256, 128), met, lines, dense, from_left, from_right,
        scratch=[
            pltpu.VMEM((4, 14, 8, 128), F32), pltpu.VMEM((4, 14, 8, 128), F32), pltpu.VMEM((3, 15, 8, 128), F32),
            pltpu.VMEM((16, 8, 128), F32), pltpu.VMEM((3, 14, 8, 128), F32),
        ],
        name="sweeps",
    )
    return out.reshape(tracers.shape)


def solution(mesh):
    split = Mesh(mesh.devices.reshape(2, 8, 2, 2, 6, 2), TILE + TRC)
    in_specs = (
        P(TRC, None, TILE, None),
        P(TRC, None, None, None, TILE, None),
        P(TRC, None, None, TILE, None),
        P(None, TILE),
        P(TILE, None),
        P(TILE, None),
        P(TILE, None, None),
    )
    out_specs = P(TRC, None, TILE, None)
    return jax.shard_map(body, mesh=split, in_specs=in_specs, out_specs=out_specs, check_vma=False)
```

time: 260 us -> 86.8 us (0.33)
  waiting for transfers between devices: 198 us -> 10.6 us
  blocking collectives: 0 us -> 38.2 us
  Pallas kernels: 0 us -> 15.7 us
  between operations: 15.6 us -> 0.03 us
  starting transfers between devices: 27.6 us -> 17.8 us
  local copies, waits for them, and re-layouts: 11.8 us -> 3.94 us
  other arithmetic: 7.12 us -> 0 us
    psum x1 -> x0, waiting for transfers between devices: 184 us -> none  [from_root(): return lax.psum(block, axis)]
    all_gather x0 -> x2, blocking collectives: none -> 38.2 us  [the longest x1 33 us: body(): pairs = lax.all_gather(mine, ('za', 'zb')).reshape(6, 2, 2, 8, 8, 128)]
    pallas_call x0 -> x6, Pallas kernels: none -> 15.7 us  [call(): pl.pallas_call(kernel, out_shape=outs, in_specs=[VM] * len(args), out_spe...]
    ppermute x4 -> x2, starting transfers between devices: 27.6 us -> 13.4 us  [the longest x1 11.5 us: body(): from_left = lax.ppermute(to_right, TILE, up)]
    ppermute x4 -> x2, waiting for transfers between devices: 13.1 us -> 8.58 us  [the longest x1 8.58 us: body(): from_right = lax.ppermute(to_left, TILE, [(b, a) for a, b in up])]
    all_to_all x0 -> x1, starting transfers between devices: none -> 4.42 us  [body(): members = lax.all_to_all(packed, ('x_lo', 'zb'), 0, 0, tiled=False)]
    scatter x3 -> x0, local copies, waits for them, and re-layouts: 3.05 us -> none  [the longest x1 1.57 us: dense_convection(): jnp.zeros((cell_total,), jnp.int32).at[column_ids].set(step_counts)]
    slice x17 -> x0, local copies, waits for them, and re-layouts: 2.68 us -> none  [the longest x12 2.07 us: pad_axis(): return jnp.pad(values_in, widths, mode=pad_mode)]
  transfers between devices with their start and end apart: 5 -> 3, of which waited for: 3 -> 2; matrix products, arithmetic and copies ran while one was open for 2% -> 1% of each run, Pallas kernels for 0% -> 2%
where the time goes in v1:
time: 86.8 us; the launch traced here: 86.3 us
  blocking collectives  38.2 us (44%)
  starting transfers between devices  17.8 us (21%)
  Pallas kernels  15.7 us (18%)
  waiting for transfers between devices  10.6 us (12%)
  local copies, waits for them, and re-layouts  3.94 us (5%)
    all_gather x1, blocking collectives, body(): pairs = lax.all_gather(mine, ('za', 'zb')).reshape(6, 2, 2, 8, 8, 128)  33 us
    pallas_call x6, Pallas kernels, call(): pl.pallas_call(kernel, out_shape=outs, in_specs=[VM] * len(args), out_spe...  15.7 us
    ppermute x1, starting transfers between devices, body(): from_left = lax.ppermute(to_right, TILE, up)  11.5 us
    ppermute x1, waiting for transfers between devices, body(): from_right = lax.ppermute(to_left, TILE, [(b, a) for a, b in up])  8.58 us
    all_gather x1, blocking collectives, body(): met = lax.all_gather(half, 'x_lo').reshape(4, 2, 8, 8, 128)  5.19 us
    all_to_all x1, starting transfers between devices, body(): members = lax.all_to_all(packed, ('x_lo', 'zb'), 0, 0, tiled=False)  4.42 us
    unnamed x10, local copies, waits for them, and re-layouts  3.94 us
    all_to_all x1, waiting for transfers between devices, body(): members = lax.all_to_all(packed, ('x_lo', 'zb'), 0, 0, tiled=False)  2.04 us
  transfers between devices with their start and end apart: 3, of which 2 were waited for; matrix products, arithmetic and copies ran while one was open for 1% of the time, Pallas kernels for 2%

profile of v1, /device:TPU:57, one launch (start us, length us, event | category | flops | bytes accessed | tf_op | source)
XLA Modules:
  0.0 86.3 jit_solution(8892317434836415921)
XLA Ops:
  0.0 1.3 %copy.9.owner_ref = s32[2,1]{1,0:T(2,128)} copy(s32[2,1]{0,1:T(1,128)} %param.10) | data formatting | bytes 16 | tf_op args[3]
  1.3 1.7 %pack.1 = (f32[4,2,8,8,128]{4,3,2,1,0:T(8,128)}, s32[2,8,128]{2,1,0:T(8,128)}) custom-call(f32[384,128]{1,0:T(8,128)} %bitcast.11, f32[128,128]{1,0:T(8,128)} %bitcast.12, s32[2,1]{1,0:T(2,128)} %copy.9.owner_ref), custom_call_target="tpu_custom_call" | custom-call | flops 20000 | bytes 262152 | tf_op jit(solution)/shard_map/pack/pallas_call | solution.py:20
  3.0 0.0 copy-start.3
  3.0 4.4 %all-to-all-start = ((f32[4,2,8,8,128]{4,3,2,1,0:T(8,128)}), f32[4,2,8,8,128]{4,3,2,1,0:T(8,128)S(1)}, u32[]{:S(2)}, u32[]{:S(2)}) async-start(f32[4,2,8,8,128]{4,3,2,1,0:T(8,128)} %get-tuple-element.10), calls=%async_computation | async-start | bytes 524288 | tf_op jit(solution)/shard_map/all_to_all | solution.py:255
  7.4 0.0 copy-done.3
  7.4 0.6 copy.12
  8.0 1.6 %convection.1.conv_ref = f32[8,8,128]{2,1,0:T(8,128)} custom-call(s32[1,256]{1,0:T(1,128)} %cols_ref.1, s32[1,256]{1,0:T(1,128)} %steps_ref.1, f32[7,256]{1,0:T(8,128)} %bitcast.13), custom_call_target="tpu_custom_call" | custom-call | flops 30000000 | bytes 9216 | tf_op jit(solution)/shard_map/convection/pallas_call | solution.py:20
  9.6 2.0 %all-to-all-done.got_ref = f32[4,2,8,8,128]{4,3,2,1,0:T(8,128)S(1)} async-done(((f32[4,2,8,8,128]{4,3,2,1,0:T(8,128)}), f32[4,2,8,8,128]{4,3,2,1,0:T(8,128)S(1)}, u32[]{:S(2)}, u32[]{:S(2)}) %all-to-all-start) | async-done | bytes 262176 | tf_op jit(solution)/shard_map/all_to_all | solution.py:255
  11.7 0.0 copy-start
  11.7 0.7 copy-done
  12.4 1.6 %pick_member.1 = f32[2,8,8,128]{3,2,1,0:T(8,128)} custom-call(s32[2,8,128]{2,1,0:T(8,128)} %get-tuple-element.9.owner_ref, f32[4,2,8,8,128]{4,3,2,1,0:T(8,128)} %copy-done), custom_call_target="tpu_custom_call" | custom-call | flops 20000 | bytes 270336 | tf_op jit(solution)/shard_map/pick_member/pallas_call | solution.py:20
  14.0 33.0 %all-gather = f32[24,8,8,128]{3,2,1,0:T(8,128)} all-gather(f32[2,8,8,128]{3,2,1,0:T(8,128)} %pick_member.1), channel_id=2, replica_groups=mesh['x_hi'=2,'y'=8,'core'=2,'x_lo'=2,'za'=6,'zb'=2] {'za','zb'}, dimensions={0}, use_global_device_ids=true | all-gather | bytes 851968 | tf_op jit(solution)/shard_map/all_gather | solution.py:260
  47.0 1.9 %pick_pair.1 = f32[2,2,8,8,128]{4,3,2,1,0:T(8,128)} custom-call(s32[2,8,128]{2,1,0:T(8,128)} %get-tuple-element.9.owner_ref, f32[6,2,2,8,8,128]{5,4,3,2,1,0:T(8,128)} %bitcast.8), custom_call_target="tpu_custom_call" | custom-call | flops 20000 | bytes 794624 | tf_op jit(solution)/shard_map/pick_pair/pallas_call | solution.py:20
  48.8 5.2 %all-gather.1.met_ref = f32[4,2,8,8,128]{4,3,2,1,0:T(8,128)} all-gather(f32[2,2,8,8,128]{4,3,2,1,0:T(8,128)} %pick_pair.1), channel_id=3, replica_groups=mesh['x_hi'=2,'y'=8,'core'=2,'x_lo'=2,'za'=6,'zb'=2] {'x_lo'}, dimensions={0}, use_global_device_ids=true | all-gather | bytes 393216 | tf_op jit(solution)/shard_map/all_gather | solution.py:262
  54.0 1.8 %send.1 = (f32[43,8,128]{2,1,0:T(8,128)}, f32[41,8,128]{2,1,0:T(8,128)}) custom-call(f32[4,2,8,8,128]{4,3,2,1,0:T(8,128)} %all-gather.1.met_ref, f32[256,128]{1,0:T(8,128)} %bitcast.9, f32[8,8,128]{2,1,0:T(8,128)} %convection.1.conv_ref), custom_call_target="tpu_custom_call" | custom-call | flops 20000 | bytes 425984 | tf_op jit(solution)/shard_map/send/pallas_call | solution.py:20
  55.8 11.5 %collective-permute-start = (f32[43,8,128]{2,1,0:T(8,128)}, f32[43,8,128]{2,1,0:T(8,128)S(1)}, u32[]{:S(2)}, u32[]{:S(2)}) collective-permute-start(f32[43,8,128]{2,1,0:T(8,128)} %get-tuple-element.11), channel_id=1, source_target_pairs={{0,24},{24,48},{48,72},{72,96},{96,120},{120,144},{144,168},{168,1... | collective-permute-start | bytes 528392 | tf_op jit(solution)/shard_map/ppermute | solution.py:269
  67.3 1.9 %collective-permute-start.1 = (f32[41,8,128]{2,1,0:T(8,128)}, f32[41,8,128]{2,1,0:T(8,128)S(1)}, u32[]{:S(2)}, u32[]{:S(2)}) collective-permute-start(f32[41,8,128]{2,1,0:T(8,128)} %get-tuple-element.12), channel_id=1, source_target_pairs={{24,0},{48,24},{72,48},{96,72},{120,96},{144,120},{168,144},{192,1... | collective-permute-start | bytes 503816 | tf_op jit(solution)/shard_map/ppermute | solution.py:270
  69.2 8.6 %collective-permute-done.1.right_ref = f32[41,8,128]{2,1,0:T(8,128)S(1)} collective-permute-done((f32[41,8,128]{2,1,0:T(8,128)}, f32[41,8,128]{2,1,0:T(8,128)S(1)}, u32[]{:S(2)}, u32[]{:S(2)}) %collective-permute-start.1) | collective-permute-done | bytes 167968 | tf_op jit(solution)/shard_map/ppermute | solution.py:270
  77.8 0.0 copy-start.2
  77.8 0.0 collective-permute-done.left_ref
  77.8 0.7 copy-done.2
  78.5 0.0 copy-start.1
  78.5 0.7 copy-done.1
  79.2 7.1 %sweeps.1 = f32[256,128]{1,0:T(8,128)} custom-call(f32[4,2,8,8,128]{4,3,2,1,0:T(8,128)} %all-gather.1.met_ref, f32[256,128]{1,0:T(8,128)} %bitcast.10, f32[8,8,128]{2,1,0:T(8,128)} %convection.1.conv_ref, f32[43,8,128]{2,1,0:T(8,128)} %copy-done.1, f32[41,8,128]{2,1,0:T(8,128)} %copy-done.2), custom_call_target="tpu_custom_call" | custom-call | flops 20000 | bytes 770048 | tf_op jit(solution)/shard_map/sweeps/pallas_call | solution.py:20
Async XLA Ops:
  3.0 4.4 %copy-start.3 = (f32[1,7,256]{2,0,1:T(1,128)S(1)}, f32[1,7,256]{2,0,1:T(1,128)}, u32[]{:S(2)}) copy-start(f32[1,7,256]{2,0,1:T(1,128)} %param.13) | copy-start | bytes 21508
  3.0 8.7 %all-to-all-start = ((f32[4,2,8,8,128]{4,3,2,1,0:T(8,128)}), f32[4,2,8,8,128]{4,3,2,1,0:T(8,128)S(1)}, u32[]{:S(2)}, u32[]{:S(2)}) async-start(f32[4,2,8,8,128]{4,3,2,1,0:T(8,128)} %get-tuple-element.10), calls=%async_computation | async-start | bytes 524288 | tf_op jit(solution)/shard_map/all_to_all | solution.py:255
  11.7 0.7 copy-start
  55.8 22.0 %collective-permute-start = (f32[43,8,128]{2,1,0:T(8,128)}, f32[43,8,128]{2,1,0:T(8,128)S(1)}, u32[]{:S(2)}, u32[]{:S(2)}) collective-permute-start(f32[43,8,128]{2,1,0:T(8,128)} %get-tuple-element.11), channel_id=1, source_target_pairs={{0,24},{24,48},{48,72},{72,96},{96,120},{120,144},{144,168},{168,1... | collective-permute-start | bytes 528392 | tf_op jit(solution)/shard_map/ppermute | solution.py:269
  67.3 10.5 %collective-permute-start.1 = (f32[41,8,128]{2,1,0:T(8,128)}, f32[41,8,128]{2,1,0:T(8,128)S(1)}, u32[]{:S(2)}, u32[]{:S(2)}) collective-permute-start(f32[41,8,128]{2,1,0:T(8,128)} %get-tuple-element.12), channel_id=1, source_target_pairs={{24,0},{48,24},{72,48},{96,72},{120,96},{144,120},{168,144},{192,1... | collective-permute-start | bytes 503816 | tf_op jit(solution)/shard_map/ppermute | solution.py:270
  77.8 0.7 copy-start.2
  78.5 0.7 copy-start.1

commit v2 on v1

--- a/solution.py
+++ b/solution.py
@@ -11,11 +11,11 @@
 F32 = jnp.float32
 
 
-def shaped(*shape):
-    return jax.ShapeDtypeStruct(shape, F32)
-
-
-def call(kernel, outs, *args, scratch=(), flops=20000, name=None):
+def shaped(*shape, dtype=F32):
+    return pltpu.VMEM(shape, dtype)
+
+
+def call(kernel, outs, *args, scratch=(), flops=20000, name=None, near=True):
     size = sum(4 * a.size for a in args)
     return pl.pallas_call(
         kernel,
@@ -25,7 +25,7 @@
         scratch_shapes=list(scratch),
         cost_estimate=pl.CostEstimate(flops=flops, bytes_accessed=size, transcendentals=0),
         name=name,
-    )(*args)
+    )(*[pltpu.with_memory_space_constraint(a, pltpu.VMEM) if near else a for a in args])
 
 
 def column(ref, first, x):
@@ -38,7 +38,7 @@
             for f in range(3):
                 out_ref[f, s, x] = column(flux_ref, (s * 3 + f) * 64, x)
             out_ref[3, s, x] = column(mass_ref, s * 64, x)
-        owner_out[s] = jnp.broadcast_to(owner_ref[s : s + 1, 0:1], (8, 128))
+        owner_out[s] = jnp.broadcast_to(owner_ref[0:1, s : s + 1], (8, 128))
 
 
 def pick_member_kernel(owner_ref, got_ref, out_ref):
@@ -68,7 +68,7 @@
 def convection_kernel(cols_ref, steps_ref, rate_ref, out_ref):
     cols = cols_ref[...]
     at_x, at_y = cols // 128, cols % 128
-    values = jnp.concatenate([steps_ref[...].astype(F32), rate_ref[...]], axis=0)
+    values = jnp.concatenate([steps_ref[...].astype(F32), rate_ref[:, 0, :]], axis=0)
     weights = jnp.concatenate([jnp.where(at_x == x, values, 0.0) for x in range(8)], axis=0)
     hot = jnp.where(lax.broadcasted_iota(jnp.int32, (128, cols.shape[1]), 0) == at_y, 1.0, 0.0)
     dense = lax.dot_general(
@@ -79,37 +79,23 @@
 
 
 FX, FY, FZ, MASS = range(4)
-RIGHT = [(FX, 0, (4, 5, 6, 7)), (MASS, 0, (4, 5, 6, 7)), (FY, 0, (5, 6, 7)), (FZ, 0, (5, 6, 7)), (FX, 1, (7,)), (MASS, 1, (7,))]
-LEFT = [(FX, 0, (0, 1, 2)), (MASS, 0, (0, 1, 2, 3)), (FY, 0, (0, 1, 2)), (FZ, 0, (0, 1, 2)), (MASS, 1, (0,))]
-
-
-def places(plan, offset):
-    at, where = 24, {}
-    for field, step, columns in plan:
-        for x in columns:
-            where[field, step, x + offset] = at
-            at += 1
-    return where, at
-
-
-FROM_LEFT, CONV_FROM_LEFT = places(RIGHT, -8)
-FROM_RIGHT, CONV_FROM_RIGHT = places(LEFT, 8)
-
-
-def send_kernel(met_ref, tracers_ref, conv_ref, right_ref, left_ref):
-    for i in range(4):
-        for n in range(6):
-            right_ref[6 * i + n] = column(tracers_ref, 64 * i, 2 + n)
-            left_ref[6 * i + n] = column(tracers_ref, 64 * i, n)
-    for plan, out, conv_columns in ((RIGHT, right_ref, (5, 6, 7)), (LEFT, left_ref, (0, 1, 2))):
+HALO = [(FX, 0, 4), (MASS, 0, 4), (FY, 0, 3), (FZ, 0, 3), (FX, 1, 1), (MASS, 1, 1)]
+SENT = 24 + sum(k for _, _, k in HALO) + 3
+
+
+def send_kernel(met_ref, tracers_ref, conv_ref, far_ref, mate_ref):
+    core = lax.axis_index("core")
+    for out, last in ((far_ref, core), (mate_ref, 1 - core)):
+        for i in range(4):
+            for n in range(6):
+                out[6 * i + n] = column(tracers_ref, 64 * i, 2 * last + n)
         at = 24
-        for field, step, columns in plan:
-            for x in columns:
-                out[at] = met_ref[field, step, x]
-                at += 1
-        for x in conv_columns:
-            out[at] = conv_ref[x]
-            at += 1
+        for field, step, k in HALO:
+            for n in range(k):
+                out[at + n] = met_ref[field, step, (8 - k) * last + n]
+            at += k
+        for n in range(3):
+            out[at + n] = conv_ref[5 * last + n]
 
 
 def clipped(value, bound):
@@ -154,50 +140,48 @@
     return q - (transport - behind(transport)) * per_mass
 
 
-def sweeps_kernel(met_ref, tracers_ref, conv_ref, left_ref, right_ref, out_ref, state, swept, factors, per_mass, lines):
+def sweeps_kernel(
+    met_ref, tracers_ref, conv_ref, far_ref, mate_ref, out_ref,
+    cells, fx_0, mass_0, fy_0, fz_0, fx_1, mass_1, tables, state, swept, factors, per_mass,
+):
     lane = lax.broadcasted_iota(jnp.int32, (8, 128), 1)
     level = lax.broadcasted_iota(jnp.int32, (8, 128), 0)
     open_y, open_z = lane < 127, level < 7
-
-    def met(field, step, x):
-        if x < 0:
-            return left_ref[FROM_LEFT[field, step, x]]
-        if x > 7:
-            return right_ref[FROM_RIGHT[field, step, x]]
-        return met_ref[field, step, x]
-
-    def dense(x):
-        if x < 0:
-            return left_ref[CONV_FROM_LEFT + 3 + x]
-        if x > 7:
-            return right_ref[CONV_FROM_RIGHT + x - 8]
-        return conv_ref[x]
-
-    def tracer(i, x):
-        if x < 0:
-            return left_ref[6 * i + 6 + x]
-        if x > 7:
-            return right_ref[6 * i + x - 8]
-        return column(tracers_ref, 64 * i, x)
+    core = lax.axis_index("core")
+
+    wide = {(FX, 0): fx_0, (MASS, 0): mass_0, (FY, 0): fy_0, (FZ, 0): fz_0, (FX, 1): fx_1, (MASS, 1): mass_1}
+    for got, right in ((far_ref, core), (mate_ref, 1 - core)):
+        for i in range(4):
+            for n in range(6):
+                cells[i, 14 * right + n] = got[6 * i + n]
+        at = 24
+        for field, step, k in HALO:
+            for n in range(k):
+                wide[field, step][(8 + k) * right + n] = got[at + n]
+            at += k
+        for n in range(3):
+            tables[11 * right + n] = got[at + n]
+    for x in range(8):
+        for i in range(4):
+            cells[i, 6 + x] = column(tracers_ref, 64 * i, x)
+        for field, step, k in HALO:
+            wide[field, step][k + x] = met_ref[field, step, x]
+        tables[3 + x] = conv_ref[x]
 
     for step in range(2):
         lo, hi = (-3, 10) if step == 0 else (0, 7)
         count = hi - lo + 1
         for n in range(count + 2):
-            per_mass[n] = 1.0 / met(MASS, step, lo - 1 + n)
+            per_mass[n] = 1.0 / wide[MASS, step][n]
         for n in range(count + 1):
-            flux = met(FX, step, lo - 1 + n)
+            flux = wide[FX, step][n]
             k1, k2 = face_factors(flux, per_mass[n], per_mass[n + 1])
             factors[0, n], factors[1, n], factors[2, n] = flux, k1, k2
-        for n in range(count):
-            lines[0, n] = met(FY, step, lo + n)
-            lines[1, n] = met(FZ, step, lo + n)
-            lines[2, n] = dense(lo + n)
 
         for i in range(4):
             q, diff, u, v, sent = {}, {}, {}, {}, {}
             for e in range(lo - 3, hi + 4):
-                q[e] = tracer(i, e) if step == 0 else state[i, e + 3]
+                q[e] = cells[i, e + 6] if step == 0 else state[i, e + 3]
                 if e - 1 in q:
                     diff[e - 1] = q[e] - q[e - 1]
                 if e - 3 in diff:
@@ -223,11 +207,11 @@
             for m in range(2):
                 n = 2 * block + m
                 r = per_mass[n + 1]
-                fy = jnp.where(open_y, lines[0, n], 0.0)
+                fy = jnp.where(open_y, fy_0[n] if step == 0 else met_ref[FY, 1, n], 0.0)
                 y1, y2 = face_factors(fy, r, pltpu.roll(r, 127, 1))
-                fz = jnp.where(open_z, lines[1, n], 0.0)
+                fz = jnp.where(open_z, fz_0[n] if step == 0 else met_ref[FZ, 1, n], 0.0)
                 z1, z2 = face_factors(fz, r, pltpu.roll(r, 7, 0))
-                table = lines[2, n]
+                table = tables[n + 3 + lo]
                 substeps = jnp.broadcast_to(table[0:1, :], (8, 128))
                 rate = jnp.where(level > 0, table, 0.0)
                 rates = [jnp.where(substeps > least, rate, 0.0) for least in (0.5, 1.5, 2.5)]
@@ -249,31 +233,31 @@
 
 def body(tracers, flux_pool, mass_pool, owner, conv_cols, conv_steps, conv_rate):
     packed, owners = call(
-        pack_kernel, (shaped(4, 2, 8, 8, 128), jax.ShapeDtypeStruct((2, 8, 128), jnp.int32)),
-        flux_pool.reshape(384, 128), mass_pool.reshape(128, 128), owner, name="pack",
+        pack_kernel, (shaped(4, 2, 8, 8, 128), shaped(2, 8, 128, dtype=jnp.int32)),
+        flux_pool.reshape(384, 128), mass_pool.reshape(128, 128), owner.reshape(1, 2), name="pack", near=False,
     )
     members = lax.all_to_all(packed, ("x_lo", "zb"), 0, 0, tiled=False)
     dense = call(
-        convection_kernel, shaped(8, 8, 128), conv_cols, conv_steps, conv_rate[0], flops=30000000, name="convection",
+        convection_kernel, shaped(8, 8, 128), conv_cols, conv_steps, conv_rate.reshape(7, 1, 256), flops=30000000, name="convection",
     )
     mine = call(pick_member_kernel, shaped(2, 8, 8, 128), owners, members, name="pick_member")
     pairs = lax.all_gather(mine, ("za", "zb")).reshape(6, 2, 2, 8, 8, 128)
     half = call(pick_pair_kernel, shaped(2, 2, 8, 8, 128), owners, pairs, name="pick_pair")
     met = lax.all_gather(half, "x_lo").reshape(4, 2, 8, 8, 128)
     lines = tracers.reshape(256, 128)
-    to_right, to_left = call(
-        send_kernel, (shaped(CONV_FROM_LEFT + 3, 8, 128), shaped(CONV_FROM_RIGHT + 3, 8, 128)), met, lines, dense, name="send",
-    )
+    to_far, to_mate = call(send_kernel, (shaped(SENT, 8, 128), shaped(SENT, 8, 128)), met, lines, dense, name="send")
     size = lax.axis_size(TILE)
-    up = [(i, (i + 1) % size) for i in range(size)]
-    from_left = lax.ppermute(to_right, TILE, up)
-    from_right = lax.ppermute(to_left, TILE, [(b, a) for a, b in up])
+    mates = [(i, i ^ 1) for i in range(size)]
+    distant = [(i, (i + 2 * (i % 2) - 1) % size) for i in range(size)]
+    from_mate = lax.ppermute(to_mate, TILE, mates)
+    from_far = lax.ppermute(to_far, TILE, distant)
     out = call(
-        sweeps_kernel, shaped(256, 128), met, lines, dense, from_left, from_right,
-        scratch=[
-            pltpu.VMEM((4, 14, 8, 128), F32), pltpu.VMEM((4, 14, 8, 128), F32), pltpu.VMEM((3, 15, 8, 128), F32),
-            pltpu.VMEM((16, 8, 128), F32), pltpu.VMEM((3, 14, 8, 128), F32),
-        ],
+        sweeps_kernel, jax.ShapeDtypeStruct((256, 128), F32), met, lines, dense, from_far, from_mate,
+        scratch=[pltpu.VMEM((4, 20, 8, 128), F32)]
+        + [pltpu.VMEM((8 + 2 * k, 8, 128), F32) for _, _, k in HALO]
+        + [pltpu.VMEM((14, 8, 128), F32)]
+        + [pltpu.VMEM((n, m, 8, 128), F32) for n, m in ((4, 14), (4, 14), (3, 15))]
+        + [pltpu.VMEM((16, 8, 128), F32)],
         name="sweeps",
     )
     return out.reshape(tracers.shape)

time: 86.8 us -> 70.5 us (0.81)
  the two profiles are of different devices: /device:TPU:57 before, /device:TPU:4 now
where the time goes in v2:
time: 70.5 us; the launch traced here: 70.2 us
  blocking collectives  42.1 us (60%)
  starting transfers between devices  9.91 us (14%)
  waiting for transfers between devices  9.3 us (13%)
  Pallas kernels  8.12 us (12%)
    all_gather x1, blocking collectives, body(): pairs = lax.all_gather(mine, ('za', 'zb')).reshape(6, 2, 2, 8, 8, 128)  36.3 us
    pallas_call x6, Pallas kernels, call(): pl.pallas_call(kernel, out_shape=outs, in_specs=[VM] * len(args), out_spe...  8.12 us
    all_gather x1, blocking collectives, body(): met = lax.all_gather(half, 'x_lo').reshape(4, 2, 8, 8, 128)  5.77 us
    ppermute x1, waiting for transfers between devices, body(): from_far = lax.ppermute(to_far, TILE, distant)  4.86 us
    all_to_all x1, waiting for transfers between devices, body(): members = lax.all_to_all(packed, ('x_lo', 'zb'), 0, 0, tiled=False)  4.44 us
    all_to_all x1, starting transfers between devices, body(): members = lax.all_to_all(packed, ('x_lo', 'zb'), 0, 0, tiled=False)  4.41 us
    ppermute x1, starting transfers between devices, body(): from_mate = lax.ppermute(to_mate, TILE, mates)  3.59 us
    ppermute x1, starting transfers between devices, body(): from_far = lax.ppermute(to_far, TILE, distant)  1.92 us
  transfers between devices with their start and end apart: 3, of which 2 were waited for; matrix products, arithmetic and copies ran while one was open for 0% of the time, Pallas kernels for 0%

profile of v2, /device:TPU:4, one launch (start us, length us, event | category | flops | bytes accessed | tf_op | source)
XLA Modules:
  0.0 70.2 jit_solution(5030313049997325589)
XLA Ops:
  0.0 1.7 %pack.1 = (f32[4,2,8,8,128]{4,3,2,1,0:T(8,128)}, s32[2,8,128]{2,1,0:T(8,128)S(1)}) custom-call(f32[384,128]{1,0:T(8,128)} %bitcast.11, f32[128,128]{1,0:T(8,128)} %bitcast.12, s32[1,2]{1,0:T(1,128)} %bitcast.13), custom_call_target="tpu_custom_call" | custom-call | flops 20000 | bytes 262152 | tf_op jit(solution)/shard_map/pack/pallas_call | solution.py:20
  1.7 0.0 copy-start.1
  1.7 0.0 copy-start.3
  1.7 4.4 %all-to-all-start = ((f32[4,2,8,8,128]{4,3,2,1,0:T(8,128)}), f32[4,2,8,8,128]{4,3,2,1,0:T(8,128)S(1)}, u32[]{:S(2)}, u32[]{:S(2)}) async-start(f32[4,2,8,8,128]{4,3,2,1,0:T(8,128)} %get-tuple-element.10), calls=%async_computation | async-start | bytes 524288 | tf_op jit(solution)/shard_map/all_to_all | solution.py:239
  6.1 0.0 copy-start.2
  6.1 0.0 copy-done.1
  6.1 0.0 copy-done.3
  6.1 0.7 copy-done.2
  6.8 0.2 convection.1.conv_ref
  7.1 4.4 %all-to-all-done.got_ref = f32[4,2,8,8,128]{4,3,2,1,0:T(8,128)S(1)} async-done(((f32[4,2,8,8,128]{4,3,2,1,0:T(8,128)}), f32[4,2,8,8,128]{4,3,2,1,0:T(8,128)S(1)}, u32[]{:S(2)}, u32[]{:S(2)}) %all-to-all-start) | async-done | bytes 262176 | tf_op jit(solution)/shard_map/all_to_all | solution.py:239
  11.5 36.3 %all-gather = f32[24,8,8,128]{3,2,1,0:T(8,128)S(1)} all-gather(f32[2,8,8,128]{3,2,1,0:T(8,128)S(1)} %pick_member.1), channel_id=2, replica_groups=mesh['x_hi'=2,'y'=8,'core'=2,'x_lo'=2,'za'=6,'zb'=2] {'za','zb'}, dimensions={0}, use_global_device_ids=true | all-gather | bytes 851968 | tf_op jit(solution)/shard_map/all_gather | solution.py:244
  47.9 0.1 pick_pair.1
  47.9 0.0 copy-start
  47.9 5.8 %all-gather.1.met_ref = f32[4,2,8,8,128]{4,3,2,1,0:T(8,128)S(1)} all-gather(f32[2,2,8,8,128]{4,3,2,1,0:T(8,128)S(1)} %pick_pair.1), channel_id=3, replica_groups=mesh['x_hi'=2,'y'=8,'core'=2,'x_lo'=2,'za'=6,'zb'=2] {'x_lo'}, dimensions={0}, use_global_device_ids=true | all-gather | bytes 393216 | tf_op jit(solution)/shard_map/all_gather | solution.py:246
  53.7 0.0 copy-done
  53.8 1.9 %collective-permute-start = (f32[43,8,128]{2,1,0:T(8,128)S(1)}, f32[43,8,128]{2,1,0:T(8,128)S(1)}, u32[]{:S(2)}, u32[]{:S(2)}) collective-permute-start(f32[43,8,128]{2,1,0:T(8,128)S(1)} %get-tuple-element.11), channel_id=1, source_target_pairs={{0,744},{24,48},{48,24},{72,96},{96,72},{120,144},{144,120},{168,1... | collective-permute-start | bytes 528392 | tf_op jit(solution)/shard_map/ppermute | solution.py:253
  55.7 3.6 %collective-permute-start.1 = (f32[43,8,128]{2,1,0:T(8,128)S(1)}, f32[43,8,128]{2,1,0:T(8,128)S(1)}, u32[]{:S(2)}, u32[]{:S(2)}) collective-permute-start(f32[43,8,128]{2,1,0:T(8,128)S(1)} %get-tuple-element.12), channel_id=1, source_target_pairs={{0,24},{24,0},{48,72},{72,48},{96,120},{120,96},{144,168},{168,144... | collective-permute-start | bytes 528392 | tf_op jit(solution)/shard_map/ppermute | solution.py:252
  59.3 4.9 %collective-permute-done.far_ref = f32[43,8,128]{2,1,0:T(8,128)S(1)} collective-permute-done((f32[43,8,128]{2,1,0:T(8,128)S(1)}, f32[43,8,128]{2,1,0:T(8,128)S(1)}, u32[]{:S(2)}, u32[]{:S(2)}) %collective-permute-start) | collective-permute-done | bytes 176160 | tf_op jit(solution)/shard_map/ppermute | solution.py:253
  64.1 0.0 collective-permute-done.1.mate_ref
  64.1 6.0 %sweeps.1 = f32[256,128]{1,0:T(8,128)} custom-call(f32[4,2,8,8,128]{4,3,2,1,0:T(8,128)S(1)} %all-gather.1.met_ref, f32[256,128]{1,0:T(8,128)S(1)} %bitcast.9, f32[8,8,128]{2,1,0:T(8,128)S(1)} %convection.1.conv_ref, f32[43,8,128]{2,1,0:T(8,128)S(1)} %collective-permute-done.far_ref, f32[43,8,128]{2,1,0:T(8,128)S(1)} %collective-permute-done.1.mate_ref), custom_call_target="tpu_custom_call" | custom-call | flops 20000 | bytes 778240 | tf_op jit(solution)/shard_map/sweeps/pallas_call | solution.py:20
  (2 shorter events, 0.1 us)
Async XLA Ops:
  1.7 4.4 %copy-start.1 = (f32[1,7,256]{2,0,1:T(1,128)S(1)}, f32[1,7,256]{2,0,1:T(1,128)}, u32[]{:S(2)}) copy-start(f32[1,7,256]{2,0,1:T(1,128)} %param.13) | copy-start | bytes 21508
  1.7 4.4 %copy-start.3 = (s32[1,256]{1,0:T(1,128)S(1)}, s32[1,256]{1,0:T(1,128)}, u32[]{:S(2)}) copy-start(s32[1,256]{1,0:T(1,128)} %steps_ref.1) | copy-start | bytes 3076
  1.7 9.8 %all-to-all-start = ((f32[4,2,8,8,128]{4,3,2,1,0:T(8,128)}), f32[4,2,8,8,128]{4,3,2,1,0:T(8,128)S(1)}, u32[]{:S(2)}, u32[]{:S(2)}) async-start(f32[4,2,8,8,128]{4,3,2,1,0:T(8,128)} %get-tuple-element.10), calls=%async_computation | async-start | bytes 524288 | tf_op jit(solution)/shard_map/all_to_all | solution.py:239
  6.1 0.7 copy-start.2
  47.9 5.8 %copy-start = (f32[4,8,8,128]{3,2,1,0:T(8,128)S(1)}, f32[4,8,8,128]{3,2,1,0:T(8,128)}, u32[]{:S(2)}) copy-start(f32[4,8,8,128]{3,2,1,0:T(8,128)} %param.7) | copy-start | bytes 393220
  53.8 10.4 %collective-permute-start = (f32[43,8,128]{2,1,0:T(8,128)S(1)}, f32[43,8,128]{2,1,0:T(8,128)S(1)}, u32[]{:S(2)}, u32[]{:S(2)}) collective-permute-start(f32[43,8,128]{2,1,0:T(8,128)S(1)} %get-tuple-element.11), channel_id=1, source_target_pairs={{0,744},{24,48},{48,24},{72,96},{96,72},{120,144},{144,120},{168,1... | collective-permute-start | bytes 528392 | tf_op jit(solution)/shard_map/ppermute | solution.py:253
  55.7 8.5 %collective-permute-start.1 = (f32[43,8,128]{2,1,0:T(8,128)S(1)}, f32[43,8,128]{2,1,0:T(8,128)S(1)}, u32[]{:S(2)}, u32[]{:S(2)}) collective-permute-start(f32[43,8,128]{2,1,0:T(8,128)S(1)} %get-tuple-element.12), channel_id=1, source_target_pairs={{0,24},{24,0},{48,72},{72,48},{96,120},{120,96},{144,168},{168,144... | collective-permute-start | bytes 528392 | tf_op jit(solution)/shard_map/ppermute | solution.py:252

commit v3 on v2

--- a/solution.py
+++ b/solution.py
@@ -6,7 +6,7 @@
 from jax.sharding import Mesh, PartitionSpec as P
 
 TILE = ("x_hi", "y", "core")
-TRC = ("x_lo", "za", "zb")
+TRC = ("x_lo", "z")
 VM = pl.BlockSpec(memory_space=pltpu.VMEM)
 F32 = jnp.float32
 
@@ -32,37 +32,29 @@
     return ref[pl.ds(first + x, 8, stride=8), :]
 
 
+MEMBERS, SHARE = 24, 3
+
+
 def pack_kernel(flux_ref, mass_ref, owner_ref, out_ref, owner_out):
     for s in range(2):
         for x in range(8):
             for f in range(3):
-                out_ref[f, s, x] = column(flux_ref, (s * 3 + f) * 64, x)
-            out_ref[3, s, x] = column(mass_ref, s * 64, x)
+                out_ref[32 * s + 8 * f + x] = column(flux_ref, (s * 3 + f) * 64, x)
+            out_ref[32 * s + 24 + x] = column(mass_ref, s * 64, x)
         owner_out[s] = jnp.broadcast_to(owner_ref[0:1, s : s + 1], (8, 128))
-
-
-def pick_member_kernel(owner_ref, got_ref, out_ref):
-    for s in range(2):
-        owner = owner_ref[s]
-        member = 2 * (owner // 12) + (owner % 2)
-        masks = [member == m for m in range(3)]
-        for x in range(8):
-            value = got_ref[3, s, x]
-            for m in range(3):
-                value = jnp.where(masks[m], got_ref[m, s, x], value)
-            out_ref[s, x] = value
-
-
-def pick_pair_kernel(owner_ref, got_ref, out_ref):
-    for s in range(2):
-        pair = (owner_ref[s] % 12) // 2
-        masks = [pair == p for p in range(5)]
-        for b in range(2):
-            for x in range(8):
-                value = got_ref[5, b, s, x]
-                for p in range(5):
-                    value = jnp.where(masks[p], got_ref[p, b, s, x], value)
-                out_ref[b, s, x] = value
+    for n in range(64, MEMBERS * SHARE):
+        out_ref[n] = jnp.zeros((8, 128), F32)
+
+
+def pick_kernel(owner_ref, got_ref, out_ref):
+    me = lax.axis_index(TRC)
+    for n in range(SHARE):
+        owner = jnp.where(SHARE * me + n < 32, owner_ref[0], owner_ref[1])
+        value = got_ref[n]
+        for m in range(1, MEMBERS):
+            value = jnp.where(owner == m, got_ref[SHARE * m + n], value)
+        for m in range(MEMBERS):
+            out_ref[SHARE * m + n] = value
 
 
 def convection_kernel(cols_ref, steps_ref, rate_ref, out_ref):
@@ -92,7 +84,7 @@
         at = 24
         for field, step, k in HALO:
             for n in range(k):
-                out[at + n] = met_ref[field, step, (8 - k) * last + n]
+                out[at + n] = met_ref[32 * step + 8 * field + (8 - k) * last + n]
             at += k
         for n in range(3):
             out[at + n] = conv_ref[5 * last + n]
@@ -165,7 +157,7 @@
         for i in range(4):
             cells[i, 6 + x] = column(tracers_ref, 64 * i, x)
         for field, step, k in HALO:
-            wide[field, step][k + x] = met_ref[field, step, x]
+            wide[field, step][k + x] = met_ref[32 * step + 8 * field + x]
         tables[3 + x] = conv_ref[x]
 
     for step in range(2):
@@ -207,9 +199,9 @@
             for m in range(2):
                 n = 2 * block + m
                 r = per_mass[n + 1]
-                fy = jnp.where(open_y, fy_0[n] if step == 0 else met_ref[FY, 1, n], 0.0)
+                fy = jnp.where(open_y, fy_0[n] if step == 0 else met_ref[32 + 8 * FY + n], 0.0)
                 y1, y2 = face_factors(fy, r, pltpu.roll(r, 127, 1))
-                fz = jnp.where(open_z, fz_0[n] if step == 0 else met_ref[FZ, 1, n], 0.0)
+                fz = jnp.where(open_z, fz_0[n] if step == 0 else met_ref[32 + 8 * FZ + n], 0.0)
                 z1, z2 = face_factors(fz, r, pltpu.roll(r, 7, 0))
                 table = tables[n + 3 + lo]
                 substeps = jnp.broadcast_to(table[0:1, :], (8, 128))
@@ -232,18 +224,17 @@
 
 
 def body(tracers, flux_pool, mass_pool, owner, conv_cols, conv_steps, conv_rate):
+    tiles = MEMBERS * SHARE
     packed, owners = call(
-        pack_kernel, (shaped(4, 2, 8, 8, 128), shaped(2, 8, 128, dtype=jnp.int32)),
+        pack_kernel, (shaped(tiles, 8, 128), shaped(2, 8, 128, dtype=jnp.int32)),
         flux_pool.reshape(384, 128), mass_pool.reshape(128, 128), owner.reshape(1, 2), name="pack", near=False,
     )
-    members = lax.all_to_all(packed, ("x_lo", "zb"), 0, 0, tiled=False)
+    dealt = lax.all_to_all(packed, TRC, 0, 0, tiled=True)
     dense = call(
         convection_kernel, shaped(8, 8, 128), conv_cols, conv_steps, conv_rate.reshape(7, 1, 256), flops=30000000, name="convection",
     )
-    mine = call(pick_member_kernel, shaped(2, 8, 8, 128), owners, members, name="pick_member")
-    pairs = lax.all_gather(mine, ("za", "zb")).reshape(6, 2, 2, 8, 8, 128)
-    half = call(pick_pair_kernel, shaped(2, 2, 8, 8, 128), owners, pairs, name="pick_pair")
-    met = lax.all_gather(half, "x_lo").reshape(4, 2, 8, 8, 128)
+    picked = call(pick_kernel, shaped(tiles, 8, 128), owners, dealt, name="pick")
+    met = lax.all_to_all(picked, TRC, 0, 0, tiled=True)
     lines = tracers.reshape(256, 128)
     to_far, to_mate = call(send_kernel, (shaped(SENT, 8, 128), shaped(SENT, 8, 128)), met, lines, dense, name="send")
     size = lax.axis_size(TILE)
@@ -264,7 +255,7 @@
 
 
 def solution(mesh):
-    split = Mesh(mesh.devices.reshape(2, 8, 2, 2, 6, 2), TILE + TRC)
+    split = Mesh(mesh.devices.reshape(2, 8, 2, 2, 12), TILE + TRC)
     in_specs = (
         P(TRC, None, TILE, None),
         P(TRC, None, None, None, TILE, None),

time: 70.5 us -> 72.6 us (1.030)
  waiting for transfers between devices: 9.3 us -> 20.4 us
  blocking collectives: 42.1 us -> 33.1 us
    all_gather x2 -> x0, blocking collectives: 42.1 us -> none  [the longest x1 36.3 us: body(): pairs = lax.all_gather(mine, ('za', 'zb')).reshape(6, 2, 2, 8, 8, 128)]
    all_to_all x0 -> x1, blocking collectives: none -> 33.1 us  [body(): dealt = lax.all_to_all(packed, TRC, 0, 0, tiled=True)]
    all_to_all x1, waiting for transfers between devices: 4.44 us -> 15.6 us  [body(): met = lax.all_to_all(picked, TRC, 0, 0, tiled=True)]
    pallas_call x6 -> x5, Pallas kernels: 8.12 us -> 8.15 us  [call(): pl.pallas_call(kernel, out_shape=outs, in_specs=[VM] * len(args), out_spe...]
where the time goes in v3:
time: 72.6 us; the launch traced here: 72.3 us
  blocking collectives  33.1 us (46%)
  waiting for transfers between devices  20.4 us (28%)
  starting transfers between devices  9.82 us (14%)
  Pallas kernels  8.15 us (11%)
    all_to_all x1, blocking collectives, body(): dealt = lax.all_to_all(packed, TRC, 0, 0, tiled=True)  33.1 us
    all_to_all x1, waiting for transfers between devices, body(): met = lax.all_to_all(picked, TRC, 0, 0, tiled=True)  15.6 us
    pallas_call x5, Pallas kernels, call(): pl.pallas_call(kernel, out_shape=outs, in_specs=[VM] * len(args), out_spe...  8.15 us
    ppermute x1, waiting for transfers between devices, body(): from_far = lax.ppermute(to_far, TILE, distant)  4.86 us
    all_to_all x1, starting transfers between devices, body(): met = lax.all_to_all(picked, TRC, 0, 0, tiled=True)  4.31 us
    ppermute x1, starting transfers between devices, body(): from_mate = lax.ppermute(to_mate, TILE, mates)  3.59 us
    ppermute x1, starting transfers between devices, body(): from_far = lax.ppermute(to_far, TILE, distant)  1.92 us
  transfers between devices with their start and end apart: 3, of which 2 were waited for; matrix products, arithmetic and copies ran while one was open for 0% of the time, Pallas kernels for 0%

profile of v3, /device:TPU:4, one launch (start us, length us, event | category | flops | bytes accessed | tf_op | source)
XLA Modules:
  0.0 72.3 jit_solution(11228202882034687457)
XLA Ops:
  0.0 1.1 %pack.1 = (f32[72,8,128]{2,1,0:T(8,128)S(1)}, s32[2,8,128]{2,1,0:T(8,128)S(1)}) custom-call(f32[384,128]{1,0:T(8,128)} %bitcast.9, f32[128,128]{1,0:T(8,128)} %bitcast.10, s32[1,2]{1,0:T(1,128)} %bitcast.11), custom_call_target="tpu_custom_call" | custom-call | flops 20000 | bytes 262152 | tf_op jit(solution)/shard_map/pack/pallas_call | solution.py:20
  1.1 33.1 %all_to_all.10.got_ref = f32[72,8,128]{2,1,0:T(8,128)S(1)} all-to-all(f32[72,8,128]{2,1,0:T(8,128)S(1)} %get-tuple-element.10), channel_id=1, replica_groups=mesh['x_hi'=2,'y'=8,'core'=2,'x_lo'=2,'z'=12] {'x_lo','z'}, dimensions={0} | all-to-all | bytes 589824 | tf_op jit(solution)/shard_map/all_to_all | solution.py:232
  34.2 0.8 %pick.1 = f32[72,8,128]{2,1,0:T(8,128)} custom-call(s32[2,8,128]{2,1,0:T(8,128)S(1)} %get-tuple-element.9.owner_ref, f32[72,8,128]{2,1,0:T(8,128)S(1)} %all_to_all.10.got_ref), custom_call_target="tpu_custom_call" | custom-call | flops 20000 | bytes 303104 | tf_op jit(solution)/shard_map/pick/pallas_call | solution.py:20
  35.0 0.0 copy-start.1
  35.0 0.0 copy-start.3
  35.0 0.0 copy-start
  35.0 4.3 %all-to-all-start.1 = ((f32[72,8,128]{2,1,0:T(8,128)}), f32[72,8,128]{2,1,0:T(8,128)S(1)}, u32[]{:S(2)}, u32[]{:S(2)}) async-start(f32[72,8,128]{2,1,0:T(8,128)} %pick.1), calls=%async_computation.1 | async-start | bytes 589824 | tf_op jit(solution)/shard_map/all_to_all | solution.py:237
  39.3 0.0 copy-start.2
  39.3 0.0 copy-done.1
  39.3 0.0 copy-done.3
  39.3 0.7 copy-done.2
  40.0 0.2 convection.1.conv_ref
  40.2 15.6 %all-to-all-done.1.met_ref = f32[72,8,128]{2,1,0:T(8,128)S(1)} async-done(((f32[72,8,128]{2,1,0:T(8,128)}), f32[72,8,128]{2,1,0:T(8,128)S(1)}, u32[]{:S(2)}, u32[]{:S(2)}) %all-to-all-start.1) | async-done | bytes 294944 | tf_op jit(solution)/shard_map/all_to_all | solution.py:237
  55.8 0.0 copy-done
  55.9 1.9 %collective-permute-start = (f32[43,8,128]{2,1,0:T(8,128)S(1)}, f32[43,8,128]{2,1,0:T(8,128)S(1)}, u32[]{:S(2)}, u32[]{:S(2)}) collective-permute-start(f32[43,8,128]{2,1,0:T(8,128)S(1)} %get-tuple-element.11), channel_id=1, source_target_pairs={{0,744},{24,48},{48,24},{72,96},{96,72},{120,144},{144,120},{168,1... | collective-permute-start | bytes 528392 | tf_op jit(solution)/shard_map/ppermute | solution.py:244
  57.8 3.6 %collective-permute-start.1 = (f32[43,8,128]{2,1,0:T(8,128)S(1)}, f32[43,8,128]{2,1,0:T(8,128)S(1)}, u32[]{:S(2)}, u32[]{:S(2)}) collective-permute-start(f32[43,8,128]{2,1,0:T(8,128)S(1)} %get-tuple-element.12), channel_id=1, source_target_pairs={{0,24},{24,0},{48,72},{72,48},{96,120},{120,96},{144,168},{168,144... | collective-permute-start | bytes 528392 | tf_op jit(solution)/shard_map/ppermute | solution.py:243
  61.4 4.9 %collective-permute-done.far_ref = f32[43,8,128]{2,1,0:T(8,128)S(1)} collective-permute-done((f32[43,8,128]{2,1,0:T(8,128)S(1)}, f32[43,8,128]{2,1,0:T(8,128)S(1)}, u32[]{:S(2)}, u32[]{:S(2)}) %collective-permute-start) | collective-permute-done | bytes 176160 | tf_op jit(solution)/shard_map/ppermute | solution.py:244
  66.2 0.0 collective-permute-done.1.mate_ref
  66.2 6.0 %sweeps.1 = f32[256,128]{1,0:T(8,128)} custom-call(f32[72,8,128]{2,1,0:T(8,128)S(1)} %all-to-all-done.1.met_ref, f32[256,128]{1,0:T(8,128)S(1)} %bitcast.7, f32[8,8,128]{2,1,0:T(8,128)S(1)} %convection.1.conv_ref, f32[43,8,128]{2,1,0:T(8,128)S(1)} %collective-permute-done.far_ref, f32[43,8,128]{2,1,0:T(8,128)S(1)} %collective-permute-done.1.mate_ref), custom_call_target="tpu_custom_call" | custom-call | flops 20000 | bytes 811008 | tf_op jit(solution)/shard_map/sweeps/pallas_call | solution.py:20
  (1 shorter events, 0.0 us)
Async XLA Ops:
  35.0 4.3 %copy-start.1 = (f32[1,7,256]{2,0,1:T(1,128)S(1)}, f32[1,7,256]{2,0,1:T(1,128)}, u32[]{:S(2)}) copy-start(f32[1,7,256]{2,0,1:T(1,128)} %param.13) | copy-start | bytes 21508
  35.0 4.3 %copy-start.3 = (s32[1,256]{1,0:T(1,128)S(1)}, s32[1,256]{1,0:T(1,128)}, u32[]{:S(2)}) copy-start(s32[1,256]{1,0:T(1,128)} %steps_ref.1) | copy-start | bytes 3076
  35.0 20.8 %copy-start = (f32[4,8,8,128]{3,2,1,0:T(8,128)S(1)}, f32[4,8,8,128]{3,2,1,0:T(8,128)}, u32[]{:S(2)}) copy-start(f32[4,8,8,128]{3,2,1,0:T(8,128)} %param.7) | copy-start | bytes 393220
  35.0 20.8 %all-to-all-start.1 = ((f32[72,8,128]{2,1,0:T(8,128)}), f32[72,8,128]{2,1,0:T(8,128)S(1)}, u32[]{:S(2)}, u32[]{:S(2)}) async-start(f32[72,8,128]{2,1,0:T(8,128)} %pick.1), calls=%async_computation.1 | async-start | bytes 589824 | tf_op jit(solution)/shard_map/all_to_all | solution.py:237
  39.3 0.7 copy-start.2
  55.9 10.4 %collective-permute-start = (f32[43,8,128]{2,1,0:T(8,128)S(1)}, f32[43,8,128]{2,1,0:T(8,128)S(1)}, u32[]{:S(2)}, u32[]{:S(2)}) collective-permute-start(f32[43,8,128]{2,1,0:T(8,128)S(1)} %get-tuple-element.11), channel_id=1, source_target_pairs={{0,744},{24,48},{48,24},{72,96},{96,72},{120,144},{144,120},{168,1... | collective-permute-start | bytes 528392 | tf_op jit(solution)/shard_map/ppermute | solution.py:244
  57.8 8.5 %collective-permute-start.1 = (f32[43,8,128]{2,1,0:T(8,128)S(1)}, f32[43,8,128]{2,1,0:T(8,128)S(1)}, u32[]{:S(2)}, u32[]{:S(2)}) collective-permute-start(f32[43,8,128]{2,1,0:T(8,128)S(1)} %get-tuple-element.12), channel_id=1, source_target_pairs={{0,24},{24,0},{48,72},{72,48},{96,120},{120,96},{144,168},{168,144... | collective-permute-start | bytes 528392 | tf_op jit(solution)/shard_map/ppermute | solution.py:243

commit v4 on v3

v4 whole, which is shorter than its diff:
```python
import functools

import jax
import jax.numpy as jnp
from jax import lax
from jax.experimental import pallas as pl
from jax.experimental.pallas import tpu as pltpu
from jax.sharding import Mesh, PartitionSpec as P

TILE = ("x_hi", "y", "core")
TRC = ("x_lo", "za", "zb")
NEAR = ("x_lo", "zb")
VM = pl.BlockSpec(memory_space=pltpu.VMEM)
F32 = jnp.float32


def shaped(*shape, dtype=F32):
    return pltpu.VMEM(shape, dtype)


def call(kernel, outs, *args, scratch=(), flops=20000, near=True):
    size = sum(4 * a.size for a in args)
    return pl.pallas_call(
        kernel,
        out_shape=outs,
        in_specs=[VM] * len(args),
        out_specs=jax.tree.map(lambda _: VM, outs),
        scratch_shapes=list(scratch),
        cost_estimate=pl.CostEstimate(flops=flops, bytes_accessed=size, transcendentals=0),
    )(*[pltpu.with_memory_space_constraint(a, pltpu.VMEM) if near else a for a in args])


def column(ref, first, x):
    return ref[pl.ds(first + x, 8, stride=8), :]


def pack_kernel(flux_ref, mass_ref, owner_ref, cols_ref, steps_ref, rate_ref, out_ref, owner_out, dense_ref):
    for s in range(2):
        for x in range(8):
            for f in range(3):
                out_ref[32 * s + 8 * f + x] = column(flux_ref, (s * 3 + f) * 64, x)
            out_ref[32 * s + 24 + x] = column(mass_ref, s * 64, x)
    first = lax.axis_index("x_lo") == 0
    owner = jnp.broadcast_to(jnp.where(first, owner_ref[0:1, 0:1], owner_ref[0:1, 1:2]), (8, 128))
    owner_out[0] = 4 * (owner // 12) + owner % 4
    owner_out[1] = (owner % 12) // 4
    cols = cols_ref[...]
    at_x, at_y = cols // 128, cols % 128
    values = jnp.concatenate([steps_ref[...].astype(F32), rate_ref[:, 0, :]], axis=0)
    weights = jnp.concatenate([jnp.where(at_x == x, values, 0.0) for x in range(8)], axis=0)
    hot = jnp.where(lax.broadcasted_iota(jnp.int32, (128, cols.shape[1]), 0) == at_y, 1.0, 0.0)
    dense = lax.dot_general(
        weights, hot, (((1,), (1,)), ((), ())),
        precision=lax.Precision.HIGHEST, preferred_element_type=F32,
    )
    dense_ref[...] = dense.reshape(dense_ref.shape)


def pick_kernel(owner_ref, got_ref, out_ref, *, which):
    owner = owner_ref[which]
    copies = out_ref.shape[0] // 8
    for n in range(8):
        value = got_ref[n]
        for m in range(1, got_ref.shape[0] // 8):
            value = jnp.where(owner == m, got_ref[8 * m + n], value)
        for m in range(copies):
            out_ref[8 * m + n] = value


FX, FY, FZ, MASS = range(4)
HALO = [(FX, 0, 4), (MASS, 0, 4), (FY, 0, 3), (FZ, 0, 3), (FX, 1, 1), (MASS, 1, 1)]
SENT = 24 + sum(k for _, _, k in HALO) + 3


def send_kernel(met_ref, tracers_ref, conv_ref, far_ref, mate_ref):
    core = lax.axis_index("core")
    for out, last in ((far_ref, core), (mate_ref, 1 - core)):
        for i in range(4):
            for n in range(6):
                out[6 * i + n] = column(tracers_ref, 64 * i, 2 * last + n)
        at = 24
        for field, step, k in HALO:
            for n in range(k):
                out[at + n] = met_ref[32 * step + 8 * field + (8 - k) * last + n]
            at += k
        for n in range(3):
            out[at + n] = conv_ref[5 * last + n]


def clipped(value, bound):
    return jnp.maximum(jnp.minimum(value, jnp.maximum(bound, 0.0)), jnp.minimum(bound, 0.0))


def edge_offset(before, here, after):
    return clipped(0.5 * here + (1.0 / 12.0) * (before - after), here)


def limited(u, v):
    return clipped(u, v + v), clipped(v, u + u)


def face_factors(flux, near, far):
    size = jnp.abs(flux)
    share = size * jnp.where(flux > 0.0, near, far)
    rest = size * (1.0 - share)
    return rest * (1.0 - share), rest * share


def line_sweep(q, flux, k1, k2, per_mass, open_face, axis):
    length = q.shape[axis]

    def ahead(x):
        return pltpu.roll(x, length - 1, axis)

    def behind(x):
        return pltpu.roll(x, 1, axis)

    q_next = ahead(q)
    diff = jnp.where(open_face, q_next - q, 0.0)
    u = edge_offset(behind(diff), diff, ahead(diff))
    v = behind(diff - u)
    u, v = limited(u, v)
    forward = flux > 0.0
    transport = (
        flux * jnp.where(forward, q, q_next)
        + k1 * jnp.where(forward, u, ahead(v))
        + k2 * jnp.where(forward, v, ahead(u))
    )
    return q - (transport - behind(transport)) * per_mass


def stage(wide, cells, tables, met_ref, tracers_ref, conv_ref, halos):
    for got, right in halos:
        if cells is not None:
            for i in range(4):
                for n in range(6):
                    cells[i, 14 * right + n] = got[6 * i + n]
            for n in range(3):
                tables[11 * right + n] = got[SENT - 3 + n]
        at = 24
        for field, step, k in HALO:
            if (field, step) in wide:
                for n in range(k):
                    wide[field, step][(8 + k) * right + n] = got[at + n]
            at += k
    for x in range(8):
        if cells is not None:
            for i in range(4):
                cells[i, 6 + x] = column(tracers_ref, 64 * i, x)
            tables[3 + x] = conv_ref[x]
        for field, step, k in HALO:
            if (field, step) in wide:
                wide[field, step][k + x] = met_ref[32 * step + 8 * field + x]


def advance(count, cell, flux_x, mass, flux_y, flux_z, table, emit, swept, factors, per_mass, group=2):
    lane = lax.broadcasted_iota(jnp.int32, (8, 128), 1)
    level = lax.broadcasted_iota(jnp.int32, (8, 128), 0)
    open_y, open_z = lane < 127, level < 7
    for n in range(count + 2):
        per_mass[n] = 1.0 / mass(n)
    for n in range(count + 1):
        flux = flux_x(n)
        k1, k2 = face_factors(flux, per_mass[n], per_mass[n + 1])
        factors[0, n], factors[1, n], factors[2, n] = flux, k1, k2

    for i in range(4):
        q, diff, u, v, sent = {}, {}, {}, {}, {}
        for e in range(-3, count + 3):
            q[e] = cell(i, e + 3)
            if e - 1 in q:
                diff[e - 1] = q[e] - q[e - 1]
            if e - 3 in diff:
                u[e - 2] = edge_offset(diff[e - 3], diff[e - 2], diff[e - 1])
                v[e - 1] = diff[e - 2] - u[e - 2]
            j = e - 2
            if j in v:
                u[j], v[j] = limited(u[j], v[j])
            j = e - 3
            if -1 <= j < count:
                flux = factors[0, j + 1]
                forward = flux > 0.0
                sent[j] = (
                    flux * jnp.where(forward, q[j], q[j + 1])
                    + factors[1, j + 1] * jnp.where(forward, u[j], v[j + 1])
                    + factors[2, j + 1] * jnp.where(forward, v[j], u[j + 1])
                )
            if 0 <= j < count:
                swept[i, j] = q[j] - (sent[j] - sent[j - 1]) * per_mass[j + 1]

    def across(block, _):
        for m in range(group):
            n = group * block + m
            r = per_mass[n + 1]
            fy = jnp.where(open_y, flux_y(n), 0.0)
            y1, y2 = face_factors(fy, r, pltpu.roll(r, 127, 1))
            fz = jnp.where(open_z, flux_z(n), 0.0)
            z1, z2 = face_factors(fz, r, pltpu.roll(r, 7, 0))
            dense = table(n)
            substeps = jnp.broadcast_to(dense[0:1, :], (8, 128))
            rate = jnp.where(level > 0, dense, 0.0)
            rates = [jnp.where(substeps > least, rate, 0.0) for least in (0.5, 1.5, 2.5)]
            keeps = [1.0 - pltpu.roll(part, 7, 0) for part in rates]
            for i in range(4):
                q = swept[i, n]
                q = line_sweep(q, fy, y1, y2, r, open_y, 1)
                q = line_sweep(q, fz, z1, z2, r, open_z, 0)
                for part, keep in zip(rates, keeps):
                    q = q * keep + part * pltpu.roll(q, 1, 0)
                emit(i, n, q)
        return 0

    lax.fori_loop(0, count // group, across, 0)


def near_kernel(
    met_ref, tracers_ref, conv_ref, mate_ref, out_ref,
    cells, fx_0, mass_0, fy_0, fz_0, tables, swept, factors, per_mass,
):
    core = lax.axis_index("core")
    wide = {(FX, 0): fx_0, (MASS, 0): mass_0, (FY, 0): fy_0, (FZ, 0): fz_0}
    stage(wide, cells, tables, met_ref, tracers_ref, conv_ref, ((mate_ref, 1 - core),))
    base = 6 * (1 - core)

    def emit(i, n, q):
        out_ref[i, n] = q

    advance(
        8, lambda i, n: cells[i, base + n], lambda n: fx_0[base + n], lambda n: mass_0[base + n],
        lambda n: fy_0[base + n], lambda n: fz_0[base + n], lambda n: tables[base + n], emit, swept, factors, per_mass,
    )


def far_kernel(
    met_ref, tracers_ref, conv_ref, mate_ref, far_ref, near_ref, out_ref,
    cells, fx_0, mass_0, fy_0, fz_0, fx_1, mass_1, tables, state, swept, factors, per_mass,
):
    core = lax.axis_index("core")
    wide = {(FX, 0): fx_0, (MASS, 0): mass_0, (FY, 0): fy_0, (FZ, 0): fz_0}
    stage(wide, cells, tables, met_ref, tracers_ref, conv_ref, ((far_ref, core),))
    stage({(FX, 1): fx_1, (MASS, 1): mass_1}, None, None, met_ref, None, None, ((far_ref, core), (mate_ref, 1 - core)))
    base = 8 * core

    def keep(i, n, q):
        state[i, base + n] = q

    for i in range(4):
        for n in range(8):
            state[i, 6 * (1 - core) + n] = near_ref[i, n]
    advance(
        6, lambda i, n: cells[i, base + n], lambda n: fx_0[base + n], lambda n: mass_0[base + n],
        lambda n: fy_0[base + n], lambda n: fz_0[base + n], lambda n: tables[base + n], keep, swept, factors, per_mass,
    )

    def emit(i, n, q):
        out_ref[pl.ds(64 * i + n, 8, stride=8), :] = q

    advance(
        8, lambda i, n: state[i, n], lambda n: fx_1[n], lambda n: mass_1[n],
        lambda n: met_ref[32 + 8 * FY + n], lambda n: met_ref[32 + 8 * FZ + n], lambda n: tables[3 + n], emit, swept, factors, per_mass,
    )


def body(tracers, flux_pool, mass_pool, owner, conv_cols, conv_steps, conv_rate):
    packed, owners, dense = call(
        pack_kernel, (shaped(64, 8, 128), shaped(2, 8, 128, dtype=jnp.int32), shaped(8, 8, 128)),
        flux_pool.reshape(384, 128), mass_pool.reshape(128, 128), owner.reshape(1, 2),
        conv_cols, conv_steps, conv_rate.reshape(7, 1, 256), near=False,
    )
    dealt = lax.all_to_all(packed, NEAR, 0, 0, tiled=True)
    third = call(functools.partial(pick_kernel, which=0), shaped(24, 8, 128), owners, dealt)
    thirds = lax.all_to_all(third, "za", 0, 0, tiled=True)
    own = call(functools.partial(pick_kernel, which=1), shaped(64, 8, 128), owners, thirds)
    met = lax.all_to_all(own, NEAR, 0, 0, tiled=True)
    lines = tracers.reshape(256, 128)
    to_far, to_mate = call(send_kernel, (shaped(SENT, 8, 128), shaped(SENT, 8, 128)), met, lines, dense)
    size = lax.axis_size(TILE)
    mates = [(i, i ^ 1) for i in range(size)]
    distant = [(i, (i + 2 * (i % 2) - 1) % size) for i in range(size)]
    from_mate = lax.ppermute(to_mate, TILE, mates)
    from_far = lax.ppermute(to_far, TILE, distant)
    arrays = [pltpu.VMEM((4, 20, 8, 128), F32)] + [pltpu.VMEM((8 + 2 * k, 8, 128), F32) for _, _, k in HALO[:4]]
    work = [pltpu.VMEM((4, 8, 8, 128), F32), pltpu.VMEM((3, 9, 8, 128), F32), pltpu.VMEM((10, 8, 128), F32)]
    ahead = call(
        near_kernel, shaped(4, 8, 8, 128), met, lines, dense, from_mate,
        scratch=arrays + [pltpu.VMEM((14, 8, 128), F32)] + work, flops=3000000,
    )
    out = call(
        far_kernel, jax.ShapeDtypeStruct((256, 128), F32), met, lines, dense, from_mate, from_far, ahead,
        scratch=arrays + [pltpu.VMEM((10, 8, 128), F32)] * 2 + [pltpu.VMEM((14, 8, 128), F32), pltpu.VMEM((4, 14, 8, 128), F32)] + work,
        flops=5000000,
    )
    return out.reshape(tracers.shape)


def solution(mesh):
    split = Mesh(mesh.devices.reshape(2, 8, 2, 2, 3, 4), TILE + TRC)
    in_specs = (
        P(TRC, None, TILE, None),
        P(TRC, None, None, None, TILE, None),
        P(TRC, None, None, TILE, None),
        P(None, TILE),
        P(TILE, None),
        P(TILE, None),
        P(TILE, None, None),
    )
    out_specs = P(TRC, None, TILE, None)
    return jax.shard_map(body, mesh=split, in_specs=in_specs, out_specs=out_specs, check_vma=False)
```

time: 72.6 us -> 67.5 us (0.930)
  the two profiles are of different devices: /device:TPU:4 before, /device:TPU:57 now
where the time goes in v4:
time: 67.5 us; the launch traced here: 67.2 us
  blocking collectives  46 us (68%)
  starting transfers between devices  8.77 us (13%)
  Pallas kernels  7.51 us (11%)
  waiting for transfers between devices  4.9 us (7%)
    all_to_all x1, blocking collectives, body(): thirds = lax.all_to_all(third, 'za', 0, 0, tiled=True)  18.3 us
    all_to_all x1, blocking collectives, body(): dealt = lax.all_to_all(packed, NEAR, 0, 0, tiled=True)  15.8 us
    all_to_all x1, blocking collectives, body(): met = lax.all_to_all(own, NEAR, 0, 0, tiled=True)  11.8 us
    pallas_call x6, Pallas kernels, call(): pl.pallas_call(kernel, out_shape=outs, in_specs=[VM] * len(args), out_spe...  7.51 us
    ppermute x1, starting transfers between devices, body(): from_mate = lax.ppermute(to_mate, TILE, mates)  5.3 us
    ppermute x1, waiting for transfers between devices, body(): from_far = lax.ppermute(to_far, TILE, distant)  4.9 us
    ppermute x1, starting transfers between devices, body(): from_far = lax.ppermute(to_far, TILE, distant)  3.46 us
  transfers between devices with their start and end apart: 2, of which 1 were waited for; matrix products, arithmetic and copies ran while one was open for 0% of the time, Pallas kernels for 3%

profile of v4, /device:TPU:57, one launch (start us, length us, event | category | flops | bytes accessed | tf_op | source)
XLA Modules:
  0.0 67.2 jit_solution(14014739112712300396)
XLA Ops:
  0.0 1.3 %shard_map.73 = (f32[64,8,128]{2,1,0:T(8,128)S(1)}, s32[2,8,128]{2,1,0:T(8,128)S(1)}, f32[8,8,128]{2,1,0:T(8,128)S(1)}) custom-call(f32[384,128]{1,0:T(8,128)} %bitcast.9, f32[128,128]{1,0:T(8,128)} %bitcast.10, s32[1,2]{1,0:T(1,128)} %bitcast.12, s32[1,256]{1,0:T(1,128)} %cols_ref.1, s32[1,256]{1,0:T(1,128)} %steps_ref.1, f32[7,1,256]{2,1,0:T(1,128)} %bitcast.11), custom_call_target="tpu_custom_call" | custom-call | flops 20000 | bytes 271368 | tf_op jit(solution)/shard_map/pallas_call | solution.py:23
  1.3 15.8 %all_to_all.15.got_ref = f32[64,8,128]{2,1,0:T(8,128)S(1)} all-to-all(f32[64,8,128]{2,1,0:T(8,128)S(1)} %get-tuple-element.11), channel_id=1, replica_groups=mesh['x_hi'=2,'y'=8,'core'=2,'x_lo'=2,'za'=3,'zb'=4] {'x_lo','zb'}, dimensions={0} | all-to-all | bytes 524288 | tf_op jit(solution)/shard_map/all_to_all | solution.py:270
  17.1 18.3 %all_to_all.16.got_ref = f32[24,8,128]{2,1,0:T(8,128)S(1)} all-to-all(f32[24,8,128]{2,1,0:T(8,128)S(1)} %shard_map.74), channel_id=1, replica_groups=mesh['x_hi'=2,'y'=8,'core'=2,'x_lo'=2,'za'=3,'zb'=4] {'za'}, dimensions={0} | all-to-all | bytes 196608 | tf_op jit(solution)/shard_map/all_to_all | solution.py:272
  35.5 0.0 copy-start
  35.5 11.8 %all_to_all.17.met_ref = f32[64,8,128]{2,1,0:T(8,128)S(1)} all-to-all(f32[64,8,128]{2,1,0:T(8,128)S(1)} %shard_map.75), channel_id=1, replica_groups=mesh['x_hi'=2,'y'=8,'core'=2,'x_lo'=2,'za'=3,'zb'=4] {'x_lo','zb'}, dimensions={0} | all-to-all | bytes 524288 | tf_op jit(solution)/shard_map/all_to_all | solution.py:274
  47.3 0.0 copy-done
  47.4 5.3 %collective-permute-start = (f32[43,8,128]{2,1,0:T(8,128)S(1)}, f32[43,8,128]{2,1,0:T(8,128)S(1)}, u32[]{:S(2)}, u32[]{:S(2)}) collective-permute-start(f32[43,8,128]{2,1,0:T(8,128)S(1)} %get-tuple-element.13), channel_id=1, source_target_pairs={{0,24},{24,0},{48,72},{72,48},{96,120},{120,96},{144,168},{168,144... | collective-permute-start | bytes 528392 | tf_op jit(solution)/shard_map/ppermute | solution.py:280
  52.7 3.5 %collective-permute-start.1 = (f32[43,8,128]{2,1,0:T(8,128)S(1)}, f32[43,8,128]{2,1,0:T(8,128)S(1)}, u32[]{:S(2)}, u32[]{:S(2)}) collective-permute-start(f32[43,8,128]{2,1,0:T(8,128)S(1)} %get-tuple-element.14), channel_id=1, source_target_pairs={{0,744},{24,48},{48,24},{72,96},{96,72},{120,144},{144,120},{168,1... | collective-permute-start | bytes 528392 | tf_op jit(solution)/shard_map/ppermute | solution.py:281
  56.2 0.0 collective-permute-done.mate_ref
  56.2 2.0 %shard_map.77.near_ref = f32[4,8,8,128]{3,2,1,0:T(8,128)S(1)} custom-call(f32[64,8,128]{2,1,0:T(8,128)S(1)} %all_to_all.17.met_ref, f32[256,128]{1,0:T(8,128)S(1)} %bitcast.7, f32[8,8,128]{2,1,0:T(8,128)S(1)} %get-tuple-element.12.conv_ref, f32[43,8,128]{2,1,0:T(8,128)S(1)} %collective-permute-done.mate_ref), custom_call_target="tpu_custom_call" | custom-call | flops 3000000 | bytes 602112 | tf_op jit(solution)/shard_map/pallas_call | solution.py:23
  58.2 4.9 %collective-permute-done.1.far_ref = f32[43,8,128]{2,1,0:T(8,128)S(1)} collective-permute-done((f32[43,8,128]{2,1,0:T(8,128)S(1)}, f32[43,8,128]{2,1,0:T(8,128)S(1)}, u32[]{:S(2)}, u32[]{:S(2)}) %collective-permute-start.1) | collective-permute-done | bytes 176160 | tf_op jit(solution)/shard_map/ppermute | solution.py:281
  63.1 4.1 %shard_map.78 = f32[256,128]{1,0:T(8,128)} custom-call(f32[64,8,128]{2,1,0:T(8,128)S(1)} %all_to_all.17.met_ref, f32[256,128]{1,0:T(8,128)S(1)} %bitcast.8, f32[8,8,128]{2,1,0:T(8,128)S(1)} %get-tuple-element.12.conv_ref, f32[43,8,128]{2,1,0:T(8,128)S(1)} %collective-permute-done.mate_ref, f32[43,8,128]{2,1,0:T(8,128)S(1)} %collective-permute-done.1.far_ref, ...), custom_call_target="tpu_custom_call" | custom-call | flops 5000000 | bytes 909312 | tf_op jit(solution)/shard_map/pallas_call | solution.py:23
  (3 shorter events, 0.1 us)
Async XLA Ops:
  35.5 11.8 %copy-start = (f32[4,8,8,128]{3,2,1,0:T(8,128)S(1)}, f32[4,8,8,128]{3,2,1,0:T(8,128)}, u32[]{:S(2)}) copy-start(f32[4,8,8,128]{3,2,1,0:T(8,128)} %param.7) | copy-start | bytes 393220
  47.4 8.8 %collective-permute-start = (f32[43,8,128]{2,1,0:T(8,128)S(1)}, f32[43,8,128]{2,1,0:T(8,128)S(1)}, u32[]{:S(2)}, u32[]{:S(2)}) collective-permute-start(f32[43,8,128]{2,1,0:T(8,128)S(1)} %get-tuple-element.13), channel_id=1, source_target_pairs={{0,24},{24,0},{48,72},{72,48},{96,120},{120,96},{144,168},{168,144... | collective-permute-start | bytes 528392 | tf_op jit(solution)/shard_map/ppermute | solution.py:280
  52.7 10.4 %collective-permute-start.1 = (f32[43,8,128]{2,1,0:T(8,128)S(1)}, f32[43,8,128]{2,1,0:T(8,128)S(1)}, u32[]{:S(2)}, u32[]{:S(2)}) collective-permute-start(f32[43,8,128]{2,1,0:T(8,128)S(1)} %get-tuple-element.14), channel_id=1, source_target_pairs={{0,744},{24,48},{48,24},{72,96},{96,72},{120,144},{144,120},{168,1... | collective-permute-start | bytes 528392 | tf_op jit(solution)/shard_map/ppermute | solution.py:281

commit v5 on v4

--- a/solution.py
+++ b/solution.py
@@ -67,6 +67,10 @@
             out_ref[8 * m + n] = value
 
 
+def rows(n):
+    return pl.ds(8 * n if isinstance(n, int) else pl.multiple_of(8 * n, 8), 8), slice(None)
+
+
 FX, FY, FZ, MASS = range(4)
 HALO = [(FX, 0, 4), (MASS, 0, 4), (FY, 0, 3), (FZ, 0, 3), (FX, 1, 1), (MASS, 1, 1)]
 SENT = 24 + sum(k for _, _, k in HALO) + 3
@@ -106,14 +110,12 @@
     return rest * (1.0 - share), rest * share
 
 
-def line_sweep(q, flux, k1, k2, per_mass, open_face, axis):
-    length = q.shape[axis]
-
+def sweep_y(q, flux, k1, k2, per_mass, open_face):
     def ahead(x):
-        return pltpu.roll(x, length - 1, axis)
+        return pltpu.roll(x, 127, 1)
 
     def behind(x):
-        return pltpu.roll(x, 1, axis)
+        return pltpu.roll(x, 1, 1)
 
     q_next = ahead(q)
     diff = jnp.where(open_face, q_next - q, 0.0)
@@ -129,39 +131,69 @@
     return q - (transport - behind(transport)) * per_mass
 
 
+def sweep_z(q, faces, per_mass):
+    diff = [q[k + 1] - q[k] for k in range(7)]
+    zero = jnp.zeros_like(q[0])
+    u, v = [zero] * 8, [zero] * 8
+    edge, rest = {}, {}
+    for k in range(7):
+        slope = diff[k - 1] - diff[k + 1] if 0 < k < 6 else (-diff[1] if k == 0 else diff[5])
+        edge[k] = clipped(0.5 * diff[k] + (1.0 / 12.0) * slope, diff[k])
+        rest[k + 1] = diff[k] - edge[k]
+        if k > 0:
+            u[k], v[k] = limited(edge[k], rest[k])
+    out, before = [], None
+    for k in range(8):
+        if k < 7:
+            flux, k1, k2 = faces(k)
+            forward = flux > 0.0
+            sent = (
+                flux * jnp.where(forward, q[k], q[k + 1])
+                + k1 * jnp.where(forward, u[k], v[k + 1])
+                + k2 * jnp.where(forward, v[k], u[k + 1])
+            )
+            change = sent if before is None else sent - before
+            before = sent
+        else:
+            change = -before
+        out.append(q[k] - change * per_mass(k))
+    return out
+
+
 def stage(wide, cells, tables, met_ref, tracers_ref, conv_ref, halos):
     for got, right in halos:
         if cells is not None:
             for i in range(4):
                 for n in range(6):
-                    cells[i, 14 * right + n] = got[6 * i + n]
+                    cells[rows(20 * i + 14 * right + n)] = got[6 * i + n]
             for n in range(3):
-                tables[11 * right + n] = got[SENT - 3 + n]
+                tables[rows(11 * right + n)] = got[SENT - 3 + n]
         at = 24
         for field, step, k in HALO:
             if (field, step) in wide:
                 for n in range(k):
-                    wide[field, step][(8 + k) * right + n] = got[at + n]
+                    wide[field, step][rows((8 + k) * right + n)] = got[at + n]
             at += k
     for x in range(8):
         if cells is not None:
             for i in range(4):
-                cells[i, 6 + x] = column(tracers_ref, 64 * i, x)
-            tables[3 + x] = conv_ref[x]
+                cells[rows(20 * i + 6 + x)] = column(tracers_ref, 64 * i, x)
+            tables[rows(3 + x)] = conv_ref[x]
         for field, step, k in HALO:
             if (field, step) in wide:
-                wide[field, step][k + x] = met_ref[32 * step + 8 * field + x]
-
-
-def advance(count, cell, flux_x, mass, flux_y, flux_z, table, emit, swept, factors, per_mass, group=2):
-    lane = lax.broadcasted_iota(jnp.int32, (8, 128), 1)
-    level = lax.broadcasted_iota(jnp.int32, (8, 128), 0)
-    open_y, open_z = lane < 127, level < 7
+                wide[field, step][rows(k + x)] = met_ref[rows(32 * step + 8 * field + x)]
+
+
+def level(ref, first, k):
+    return ref[pl.ds(8 * first + k, 8, stride=8), :]
+
+
+def advance(count, shift, cell, flux_x, mass, flux_y, flux_z, tables, window, emit, swept, factors, per_mass, lines):
     for n in range(count + 2):
-        per_mass[n] = 1.0 / mass(n)
+        per_mass[rows(n + 2)] = 1.0 / mass(n)
     for n in range(count + 1):
         flux = flux_x(n)
-        k1, k2 = face_factors(flux, per_mass[n], per_mass[n + 1])
+        k1, k2 = face_factors(flux, per_mass[rows(n + 2)], per_mass[rows(n + 3)])
         factors[0, n], factors[1, n], factors[2, n] = flux, k1, k2
 
     for i in range(4):
@@ -186,78 +218,84 @@
                     + factors[2, j + 1] * jnp.where(forward, v[j], u[j + 1])
                 )
             if 0 <= j < count:
-                swept[i, j] = q[j] - (sent[j] - sent[j - 1]) * per_mass[j + 1]
-
-    def across(block, _):
-        for m in range(group):
-            n = group * block + m
-            r = per_mass[n + 1]
-            fy = jnp.where(open_y, flux_y(n), 0.0)
-            y1, y2 = face_factors(fy, r, pltpu.roll(r, 127, 1))
-            fz = jnp.where(open_z, flux_z(n), 0.0)
-            z1, z2 = face_factors(fz, r, pltpu.roll(r, 7, 0))
-            dense = table(n)
-            substeps = jnp.broadcast_to(dense[0:1, :], (8, 128))
-            rate = jnp.where(level > 0, dense, 0.0)
-            rates = [jnp.where(substeps > least, rate, 0.0) for least in (0.5, 1.5, 2.5)]
-            keeps = [1.0 - pltpu.roll(part, 7, 0) for part in rates]
-            for i in range(4):
-                q = swept[i, n]
-                q = line_sweep(q, fy, y1, y2, r, open_y, 1)
-                q = line_sweep(q, fz, z1, z2, r, open_z, 0)
-                for part, keep in zip(rates, keeps):
-                    q = q * keep + part * pltpu.roll(q, 1, 0)
-                emit(i, n, q)
-        return 0
-
-    lax.fori_loop(0, count // group, across, 0)
+                swept[rows(8 * i + j + shift)] = q[j] - (sent[j] - sent[j - 1]) * per_mass[rows(j + 3)]
+
+    open_y = lax.broadcasted_iota(jnp.int32, (8, 128), 1) < 127
+    substeps = level(tables, window, 0)
+    for k in range(8):
+        r = level(per_mass, 3 - shift, k)
+        fy = jnp.where(open_y, flux_y(k), 0.0)
+        y1, y2 = face_factors(fy, r, pltpu.roll(r, 127, 1))
+        lines[0, k], lines[1, k], lines[2, k], lines[3, k] = r, fy, y1, y2
+        if k > 0:
+            fz = flux_z(k - 1)
+            z1, z2 = face_factors(fz, r_below, r)
+            lines[4, k - 1], lines[5, k - 1], lines[6, k - 1] = fz, z1, z2
+            rate = level(tables, window, k)
+            lines[7, k] = rate
+            lines[8, k] = jnp.where(substeps > 1.5, rate, 0.0)
+            lines[9, k] = jnp.where(substeps > 2.5, rate, 0.0)
+        r_below = r
+
+    for i in range(4):
+        q = [level(swept, 8 * i, k) for k in range(8)]
+        q = [sweep_y(q[k], lines[1, k], lines[2, k], lines[3, k], lines[0, k], open_y) for k in range(8)]
+        q = sweep_z(q, lambda k: (lines[4, k], lines[5, k], lines[6, k]), lambda k: lines[0, k])
+        for m in (7, 8, 9):
+            up = [None] + [lines[m, k] for k in range(1, 8)]
+            q = [
+                (q[k] * (1.0 - up[k + 1]) if k < 7 else q[k]) + (up[k] * q[k - 1] if k > 0 else 0.0)
+                for k in range(8)
+            ]
+        for k in range(8):
+            emit(i, k, q[k])
 
 
 def near_kernel(
     met_ref, tracers_ref, conv_ref, mate_ref, out_ref,
-    cells, fx_0, mass_0, fy_0, fz_0, tables, swept, factors, per_mass,
+    cells, fx_0, mass_0, fy_0, fz_0, tables, swept, factors, per_mass, lines,
 ):
     core = lax.axis_index("core")
     wide = {(FX, 0): fx_0, (MASS, 0): mass_0, (FY, 0): fy_0, (FZ, 0): fz_0}
     stage(wide, cells, tables, met_ref, tracers_ref, conv_ref, ((mate_ref, 1 - core),))
     base = 6 * (1 - core)
 
-    def emit(i, n, q):
-        out_ref[i, n] = q
+    def emit(i, k, q):
+        out_ref[pl.ds(64 * i + k, 8, stride=8), :] = q
 
     advance(
-        8, lambda i, n: cells[i, base + n], lambda n: fx_0[base + n], lambda n: mass_0[base + n],
-        lambda n: fy_0[base + n], lambda n: fz_0[base + n], lambda n: tables[base + n], emit, swept, factors, per_mass,
+        8, 0, lambda i, n: cells[rows(20 * i + base + n)], lambda n: fx_0[rows(base + n)], lambda n: mass_0[rows(base + n)],
+        lambda k: level(fy_0, base, k), lambda k: level(fz_0, base, k), tables, base, emit, swept, factors, per_mass, lines,
     )
 
 
 def far_kernel(
     met_ref, tracers_ref, conv_ref, mate_ref, far_ref, near_ref, out_ref,
-    cells, fx_0, mass_0, fy_0, fz_0, fx_1, mass_1, tables, state, swept, factors, per_mass,
+    cells, fx_0, mass_0, fy_0, fz_0, fx_1, mass_1, tables, state, swept, factors, per_mass, lines,
 ):
     core = lax.axis_index("core")
     wide = {(FX, 0): fx_0, (MASS, 0): mass_0, (FY, 0): fy_0, (FZ, 0): fz_0}
     stage(wide, cells, tables, met_ref, tracers_ref, conv_ref, ((far_ref, core),))
     stage({(FX, 1): fx_1, (MASS, 1): mass_1}, None, None, met_ref, None, None, ((far_ref, core), (mate_ref, 1 - core)))
-    base = 8 * core
-
-    def keep(i, n, q):
-        state[i, base + n] = q
-
+    base, window = 8 * core, 6 * core
+
+    def keep(i, k, q):
+        state[pl.ds(8 * (14 * i + window) + k, 8, stride=8), :] = q
+
+    advance(
+        6, 2 * core, lambda i, n: cells[rows(20 * i + base + n)], lambda n: fx_0[rows(base + n)], lambda n: mass_0[rows(base + n)],
+        lambda k: level(fy_0, window, k), lambda k: level(fz_0, window, k), tables, window, keep, swept, factors, per_mass, lines,
+    )
     for i in range(4):
         for n in range(8):
-            state[i, 6 * (1 - core) + n] = near_ref[i, n]
+            state[rows(14 * i + 6 * (1 - core) + n)] = near_ref[rows(8 * i + n)]
+
+    def emit(i, k, q):
+        out_ref[rows(8 * i + k)] = q
+
     advance(
-        6, lambda i, n: cells[i, base + n], lambda n: fx_0[base + n], lambda n: mass_0[base + n],
-        lambda n: fy_0[base + n], lambda n: fz_0[base + n], lambda n: tables[base + n], keep, swept, factors, per_mass,
-    )
-
-    def emit(i, n, q):
-        out_ref[pl.ds(64 * i + n, 8, stride=8), :] = q
-
-    advance(
-        8, lambda i, n: state[i, n], lambda n: fx_1[n], lambda n: mass_1[n],
-        lambda n: met_ref[32 + 8 * FY + n], lambda n: met_ref[32 + 8 * FZ + n], lambda n: tables[3 + n], emit, swept, factors, per_mass,
+        8, 0, lambda i, n: state[rows(14 * i + n)], lambda n: fx_1[rows(n)], lambda n: mass_1[rows(n)],
+        lambda k: level(met_ref, 32 + 8 * FY, k), lambda k: level(met_ref, 32 + 8 * FZ, k), tables, 3, emit, swept, factors, per_mass, lines,
     )
 
 
@@ -279,16 +317,20 @@
     distant = [(i, (i + 2 * (i % 2) - 1) % size) for i in range(size)]
     from_mate = lax.ppermute(to_mate, TILE, mates)
     from_far = lax.ppermute(to_far, TILE, distant)
-    arrays = [pltpu.VMEM((4, 20, 8, 128), F32)] + [pltpu.VMEM((8 + 2 * k, 8, 128), F32) for _, _, k in HALO[:4]]
-    work = [pltpu.VMEM((4, 8, 8, 128), F32), pltpu.VMEM((3, 9, 8, 128), F32), pltpu.VMEM((10, 8, 128), F32)]
+
+    def columns(n):
+        return pltpu.VMEM((8 * n, 128), F32)
+
+    met = met.reshape(512, 128)
+    arrays = [columns(80)] + [columns(8 + 2 * k) for _, _, k in HALO[:4]]
+    work = [columns(32), pltpu.VMEM((3, 9, 8, 128), F32), columns(12), pltpu.VMEM((10, 8, 8, 128), F32)]
     ahead = call(
-        near_kernel, shaped(4, 8, 8, 128), met, lines, dense, from_mate,
-        scratch=arrays + [pltpu.VMEM((14, 8, 128), F32)] + work, flops=3000000,
+        near_kernel, shaped(256, 128), met, lines, dense, from_mate,
+        scratch=arrays + [columns(14)] + work, flops=3000000,
     )
     out = call(
         far_kernel, jax.ShapeDtypeStruct((256, 128), F32), met, lines, dense, from_mate, from_far, ahead,
-        scratch=arrays + [pltpu.VMEM((10, 8, 128), F32)] * 2 + [pltpu.VMEM((14, 8, 128), F32), pltpu.VMEM((4, 14, 8, 128), F32)] + work,
-        flops=5000000,
+        scratch=arrays + [columns(10)] * 2 + [columns(14), columns(56)] + work, flops=5000000,
     )
     return out.reshape(tracers.shape)
 

time: 67.5 us -> 65.4 us (0.969)
  Pallas kernels: 7.51 us -> 4.23 us
  waiting for transfers between devices: 4.9 us -> 6.12 us
    pallas_call x6, Pallas kernels: 7.51 us -> 4.23 us  [call(): pl.pallas_call(kernel, out_shape=outs, in_specs=[VM] * len(args), out_spe...]
    ppermute x1, waiting for transfers between devices: 4.9 us -> 6.12 us  [body(): from_far = lax.ppermute(to_far, TILE, distant)]
  transfers between devices with their start and end apart: 2 -> 2, of which waited for: 1 -> 1; matrix products, arithmetic and copies ran while one was open for 0% -> 0% of each run, Pallas kernels for 3% -> 1%
where the time goes in v5:
time: 65.4 us; the launch traced here: 65.1 us
  blocking collectives  46 us (70%)
  starting transfers between devices  8.77 us (13%)
  waiting for transfers between devices  6.12 us (9%)
  Pallas kernels  4.23 us (6%)
    all_to_all x1, blocking collectives, body(): thirds = lax.all_to_all(third, 'za', 0, 0, tiled=True)  18.3 us
    all_to_all x1, blocking collectives, body(): dealt = lax.all_to_all(packed, NEAR, 0, 0, tiled=True)  15.8 us
    all_to_all x1, blocking collectives, body(): met = lax.all_to_all(own, NEAR, 0, 0, tiled=True)  11.8 us
    ppermute x1, waiting for transfers between devices, body(): from_far = lax.ppermute(to_far, TILE, distant)  6.12 us
    ppermute x1, starting transfers between devices, body(): from_mate = lax.ppermute(to_mate, TILE, mates)  5.3 us
    pallas_call x6, Pallas kernels, call(): pl.pallas_call(kernel, out_shape=outs, in_specs=[VM] * len(args), out_spe...  4.23 us
    ppermute x1, starting transfers between devices, body(): from_far = lax.ppermute(to_far, TILE, distant)  3.46 us
  transfers between devices with their start and end apart: 2, of which 1 were waited for; matrix products, arithmetic and copies ran while one was open for 0% of the time, Pallas kernels for 1%

profile of v5, /device:TPU:57, one launch (start us, length us, event | category | flops | bytes accessed | tf_op | source)
XLA Modules:
  0.0 65.1 jit_solution(12161548534393959420)
XLA Ops:
  0.0 1.3 %shard_map.73 = (f32[64,8,128]{2,1,0:T(8,128)S(1)}, s32[2,8,128]{2,1,0:T(8,128)S(1)}, f32[8,8,128]{2,1,0:T(8,128)S(1)}) custom-call(f32[384,128]{1,0:T(8,128)} %bitcast.12, f32[128,128]{1,0:T(8,128)} %bitcast.13, s32[1,2]{1,0:T(1,128)} %bitcast.15, s32[1,256]{1,0:T(1,128)} %cols_ref.1, s32[1,256]{1,0:T(1,128)} %steps_ref.1, f32[7,1,256]{2,1,0:T(1,128)} %bitcast.14), custom_call_target="tpu_custom_call" | custom-call | flops 20000 | bytes 271368 | tf_op jit(solution)/shard_map/pallas_call | solution.py:23
  1.3 15.8 %all_to_all.15.got_ref = f32[64,8,128]{2,1,0:T(8,128)S(1)} all-to-all(f32[64,8,128]{2,1,0:T(8,128)S(1)} %get-tuple-element.11), channel_id=1, replica_groups=mesh['x_hi'=2,'y'=8,'core'=2,'x_lo'=2,'za'=3,'zb'=4] {'x_lo','zb'}, dimensions={0} | all-to-all | bytes 524288 | tf_op jit(solution)/shard_map/all_to_all | solution.py:308
  17.1 18.3 %all_to_all.16.got_ref = f32[24,8,128]{2,1,0:T(8,128)S(1)} all-to-all(f32[24,8,128]{2,1,0:T(8,128)S(1)} %shard_map.74), channel_id=1, replica_groups=mesh['x_hi'=2,'y'=8,'core'=2,'x_lo'=2,'za'=3,'zb'=4] {'za'}, dimensions={0} | all-to-all | bytes 196608 | tf_op jit(solution)/shard_map/all_to_all | solution.py:310
  35.5 0.0 copy-start
  35.5 11.8 %all_to_all.17.met_ref = f32[64,8,128]{2,1,0:T(8,128)S(1)} all-to-all(f32[64,8,128]{2,1,0:T(8,128)S(1)} %shard_map.75), channel_id=1, replica_groups=mesh['x_hi'=2,'y'=8,'core'=2,'x_lo'=2,'za'=3,'zb'=4] {'x_lo','zb'}, dimensions={0} | all-to-all | bytes 524288 | tf_op jit(solution)/shard_map/all_to_all | solution.py:312
  47.3 0.0 copy-done
  47.4 5.3 %collective-permute-start = (f32[43,8,128]{2,1,0:T(8,128)S(1)}, f32[43,8,128]{2,1,0:T(8,128)S(1)}, u32[]{:S(2)}, u32[]{:S(2)}) collective-permute-start(f32[43,8,128]{2,1,0:T(8,128)S(1)} %get-tuple-element.13), channel_id=1, source_target_pairs={{0,24},{24,0},{48,72},{72,48},{96,120},{120,96},{144,168},{168,144... | collective-permute-start | bytes 528392 | tf_op jit(solution)/shard_map/ppermute | solution.py:318
  52.7 3.5 %collective-permute-start.1 = (f32[43,8,128]{2,1,0:T(8,128)S(1)}, f32[43,8,128]{2,1,0:T(8,128)S(1)}, u32[]{:S(2)}, u32[]{:S(2)}) collective-permute-start(f32[43,8,128]{2,1,0:T(8,128)S(1)} %get-tuple-element.14), channel_id=1, source_target_pairs={{0,744},{24,48},{48,24},{72,96},{96,72},{120,144},{144,120},{168,1... | collective-permute-start | bytes 528392 | tf_op jit(solution)/shard_map/ppermute | solution.py:319
  56.2 0.0 collective-permute-done.mate_ref
  56.2 0.8 %shard_map.77.near_ref = f32[256,128]{1,0:T(8,128)S(1)} custom-call(f32[512,128]{1,0:T(8,128)S(1)} %bitcast.7, f32[256,128]{1,0:T(8,128)S(1)} %bitcast.10, f32[8,8,128]{2,1,0:T(8,128)S(1)} %get-tuple-element.12.conv_ref, f32[43,8,128]{2,1,0:T(8,128)S(1)} %collective-permute-done.mate_ref), custom_call_target="tpu_custom_call" | custom-call | flops 3000000 | bytes 602112 | tf_op jit(solution)/shard_map/pallas_call | solution.py:23
  56.9 6.1 %collective-permute-done.1.far_ref = f32[43,8,128]{2,1,0:T(8,128)S(1)} collective-permute-done((f32[43,8,128]{2,1,0:T(8,128)S(1)}, f32[43,8,128]{2,1,0:T(8,128)S(1)}, u32[]{:S(2)}, u32[]{:S(2)}) %collective-permute-start.1) | collective-permute-done | bytes 176160 | tf_op jit(solution)/shard_map/ppermute | solution.py:319
  63.1 2.1 %shard_map.78 = f32[256,128]{1,0:T(8,128)} custom-call(f32[512,128]{1,0:T(8,128)S(1)} %bitcast.8, f32[256,128]{1,0:T(8,128)S(1)} %bitcast.11, f32[8,8,128]{2,1,0:T(8,128)S(1)} %get-tuple-element.12.conv_ref, f32[43,8,128]{2,1,0:T(8,128)S(1)} %collective-permute-done.mate_ref, f32[43,8,128]{2,1,0:T(8,128)S(1)} %collective-permute-done.1.far_ref, ...), custom_call_target="tpu_custom_call" | custom-call | flops 5000000 | bytes 909312 | tf_op jit(solution)/shard_map/pallas_call | solution.py:23
  (3 shorter events, 0.1 us)
Async XLA Ops:
  35.5 11.8 %copy-start = (f32[4,8,8,128]{3,2,1,0:T(8,128)S(1)}, f32[4,8,8,128]{3,2,1,0:T(8,128)}, u32[]{:S(2)}) copy-start(f32[4,8,8,128]{3,2,1,0:T(8,128)} %param.7) | copy-start | bytes 393220
  47.4 8.8 %collective-permute-start = (f32[43,8,128]{2,1,0:T(8,128)S(1)}, f32[43,8,128]{2,1,0:T(8,128)S(1)}, u32[]{:S(2)}, u32[]{:S(2)}) collective-permute-start(f32[43,8,128]{2,1,0:T(8,128)S(1)} %get-tuple-element.13), channel_id=1, source_target_pairs={{0,24},{24,0},{48,72},{72,48},{96,120},{120,96},{144,168},{168,144... | collective-permute-start | bytes 528392 | tf_op jit(solution)/shard_map/ppermute | solution.py:318
  52.7 10.4 %collective-permute-start.1 = (f32[43,8,128]{2,1,0:T(8,128)S(1)}, f32[43,8,128]{2,1,0:T(8,128)S(1)}, u32[]{:S(2)}, u32[]{:S(2)}) collective-permute-start(f32[43,8,128]{2,1,0:T(8,128)S(1)} %get-tuple-element.14), channel_id=1, source_target_pairs={{0,744},{24,48},{48,24},{72,96},{96,72},{120,144},{144,120},{168,1... | collective-permute-start | bytes 528392 | tf_op jit(solution)/shard_map/ppermute | solution.py:319
